TPU v7x, 32 devices: a whole 2x2x4 slice. The times are simulated.
32 devices in a mesh: batch: 16 (over z, x, core), mlp: 2 (over y).
Axes of the slice: x: 2, y: 2, z: 4, core: 2. Of those that a mesh axis runs over, the one named last changes fastest.
Arguments:
- inputs: bfloat16 [16384, 768], P(('batch', 'mlp')), may hold values from -6 to 6
- doc_lengths: int32 [32, 3], P(('batch', 'mlp')), may hold values from 1 to 256, 512 in all within a row
- ln1_gain: bfloat16 [768], replicated, may hold values from 0.5 to 1.5
- ln1_bias: bfloat16 [768], replicated, may hold values from -1.75 to 1.75
- attn_in: bfloat16 [768, 2304], replicated, may hold values from -0.21875 to 0.21875
- qv_bias: bfloat16 [2, 768], replicated, may hold values from -3 to 3
- attn_out: bfloat16 [768, 768], replicated, may hold values from -0.875 to 0.875
- attn_out_bias: bfloat16 [768], replicated, may hold values from -1.75 to 1.75
- ln2_gain: bfloat16 [768], replicated, may hold values from 0.5 to 1.5
- second_norm_bias: bfloat16 [768], replicated, may hold values from -1.75 to 1.75
- mlp_in: bfloat16 [768, 3072], P(None, 'mlp'), may hold values from -0.21875 to 0.21875
- mlp_in_bias: bfloat16 [3072], P('mlp'), may hold values from -3 to 3
- mlp_out: bfloat16 [3072, 768], P('mlp'), may hold values from -0.109375 to 0.109375
- mlp_out_bias: bfloat16 [768], replicated, may hold values from -1.75 to 1.75
- cotangent: bfloat16 [16384, 768], P(('batch', 'mlp')), may hold values from -6 to 6
Outputs:
- layer_output: bfloat16 [16384, 768], P(('batch', 'mlp'))
- input_grad: bfloat16 [16384, 768], P(('batch', 'mlp'))
- ln1_gain_grad: float32 [768], replicated
- ln1_bias_grad: float32 [768], replicated
- attn_in_grad: float32 [768, 2304], replicated
- qv_bias_grad: float32 [2, 768], replicated
- attn_out_grad: float32 [768, 768], replicated
- attn_out_bias_grad: float32 [768], replicated
- ln2_gain_grad: float32 [768], replicated
- ln2_bias_grad: float32 [768], replicated
- mlp_in_grad: float32 [768, 3072], P(None, 'mlp')
- perceptron_input_bias_gradient: float32 [3072], P('mlp')
- mlp_out_grad: float32 [3072, 768], P('mlp')
- mlp_out_bias_grad: float32 [768], replicated
Inputs may be any that keep to these rules, and one draw needn't show every extreme that they name: `doc_lengths`: row s holds the lengths of the 3 documents packed in segment s, in order; they sum to 512. A segment's first document continues the last document of the segment before it in its stream.
All inputs are finite; a program needn't handle non-finite values.
Results may differ from a plain program's by a relative error of at most 0.019.
Values may be sent and summed in bfloat16 or wider, within the bound.
No kernel may reach another device: no remote copies, remote signals or barrier semaphores. Data moves between devices by JAX's collectives and lax.ppermute only.
A program may use at most 192 MiB of HBM per device.

v0:
```python
import jax
import jax.numpy as jnp
from jax import lax
from jax.sharding import PartitionSpec as P

D = 768
H = 12
HD = 64
NB = 512
L = 512
NDOC = 3


highest = lax.Precision.HIGHEST


def shifted(value, axis, by):
    count = lax.axis_size(axis)
    pairs = [(i, i + by) for i in range(count) if 0 <= i + by < count]
    return lax.ppermute(value, axis, pairs)


def layer_norm(matrix, gain_row, shift_row):
    center = jnp.mean(matrix, axis=-1, keepdims=True)
    centered = matrix - center
    spread = jnp.mean(centered * centered, axis=-1, keepdims=True)
    return centered * lax.rsqrt(spread + 1e-05) * gain_row + shift_row


def norm_backward(matrix, gain_row, shift_row, upstream):
    unused, pullback = jax.vjp(layer_norm, matrix, gain_row, shift_row)
    return pullback(upstream)


def gelu_tanh(values):
    argument = 0.7978845608028654 * (values + 0.044715 * values * values * values)
    return 0.5 * values * (1.0 + jnp.tanh(argument))


def gelu_backward(values, upstream):
    unused, pullback = jax.vjp(gelu_tanh, values)
    return pullback(upstream)[0]


def soft_rows(scores):
    row_top = jnp.max(scores, axis=-1, keepdims=True)
    weights = jnp.exp(scores - row_top)
    row_total = jnp.sum(weights, axis=-1, keepdims=True)
    return (weights / row_total, row_top + jnp.log(row_total))


def basis_table(doc_lengths):
    last_len = doc_lengths[:, NDOC - 1].astype(jnp.float32)
    places = jnp.arange(L, dtype=jnp.float32)
    centers = (jnp.arange(NB, dtype=jnp.float32) + 0.5) / NB
    offsets = places[None, :] - L + last_len[:, None] + 0.5
    distances = centers[None, :, None] * last_len[:, None, None] - offsets[:, None, :]
    inside = (offsets > 0.0).astype(jnp.float32)
    weights = jnp.exp(-0.5 * distances * distances) * inside[:, None, :]
    return weights / jnp.sum(weights, axis=2, keepdims=True)


def doc_tables(doc_lengths):
    places = jnp.arange(L, dtype=jnp.int32)
    segment_bounds = jnp.cumsum(doc_lengths, axis=1)
    documents = jnp.sum(
        (places[None, :, None] >= segment_bounds[:, None, : NDOC - 1]).astype(jnp.int32), axis=2
    )
    tail_mask = places[None, :] >= (L - doc_lengths[:, NDOC - 1])[:, None]
    head_mask = places[None, :] < doc_lengths[:, 0][:, None]
    return (documents, tail_mask, head_mask)


def shards(
    inputs,
    doc_lengths,
    ln1_gain,
    ln1_bias,
    attn_in,
    qv_bias,
    attn_out,
    attn_out_bias,
    ln2_gain,
    second_norm_bias,
    mlp_in,
    mlp_in_bias,
    mlp_out,
    mlp_out_bias,
    cotangent,
):
    seg_count = doc_lengths.shape[0]
    own_rows = inputs.shape[0]
    score_scale = HD ** (-0.5)
    gain_one = ln1_gain.astype(jnp.float32)
    bias_one = ln1_bias.astype(jnp.float32)
    gain_two = ln2_gain.astype(jnp.float32)
    bias_two = second_norm_bias.astype(jnp.float32)
    activations = inputs.astype(jnp.float32)
    normed = layer_norm(activations, gain_one, bias_one).astype(jnp.bfloat16)
    documents, tail_mask, head_mask = doc_tables(doc_lengths)
    basis = basis_table(doc_lengths)
    summary = jnp.einsum(
        "sjt,std->sjd",
        basis,
        normed.reshape(seg_count, L, D).astype(jnp.float32),
        precision=highest,
    ).astype(jnp.bfloat16)
    before = shifted(summary[seg_count - 1], "mlp", 1)
    coefficients = jnp.concatenate([before[None], summary[: seg_count - 1]], axis=0)
    stream_start = (jnp.arange(seg_count) == 0) & (lax.axis_index("mlp") == 0)
    reading = (head_mask & jnp.logical_not(stream_start)[:, None]).astype(jnp.float32)
    qkv = jnp.dot(normed, attn_in, preferred_element_type=jnp.float32)
    query_h = (qkv[:, :D] + qv_bias[0]).astype(jnp.bfloat16).reshape(seg_count, L, H, HD)
    key_h = qkv[:, D : 2 * D].astype(jnp.bfloat16).reshape(seg_count, L, H, HD)
    value_h = (qkv[:, 2 * D :] + qv_bias[1]).astype(jnp.bfloat16).reshape(seg_count, L, H, HD)
    mem_kv = jnp.einsum(
        "sjd,de->sje", coefficients, attn_in[:, D:], preferred_element_type=jnp.float32
    )
    mem_key_h = mem_kv[:, :, :D].astype(jnp.bfloat16).reshape(seg_count, NB, H, HD)
    mem_value_h = (mem_kv[:, :, D:] + qv_bias[1]).astype(jnp.bfloat16).reshape(seg_count, NB, H, HD)
    places = jnp.arange(L, dtype=jnp.int32)
    causal = places[None, :] <= places[:, None]
    segment = 0
    allowed = causal & (documents[segment][:, None] == documents[segment][None, :])
    scores = (
        jnp.einsum(
            "qhd,khd->hqk", query_h[segment], key_h[segment], preferred_element_type=jnp.float32
        )
        * score_scale
    )
    scores = jnp.where(allowed[None], scores, -1000000000.0)
    weights, lse_local = soft_rows(scores)
    local_out = jnp.einsum(
        "hqk,khd->qhd",
        weights.astype(jnp.bfloat16),
        value_h[segment],
        preferred_element_type=jnp.float32,
    )
    mem_scores = (
        jnp.einsum(
            "qhd,khd->hqk", query_h[segment], mem_key_h[segment], preferred_element_type=jnp.float32
        )
        * score_scale
    )
    mem_weights, lse_memory = soft_rows(mem_scores)
    remote = jnp.einsum(
        "hqk,khd->qhd",
        mem_weights.astype(jnp.bfloat16),
        mem_value_h[segment],
        preferred_element_type=jnp.float32,
    )
    mixture_parts = (local_out + reading[segment][:, None, None] * remote).reshape(L, D)
    local_lse = [lse_local]
    memory_lse = [lse_memory]
    mixture = mixture_parts.astype(jnp.bfloat16)
    branch = jnp.dot(mixture, attn_out, preferred_element_type=jnp.float32) + attn_out_bias
    middle = activations + branch
    normed_two = layer_norm(middle, gain_two, bias_two).astype(jnp.bfloat16)
    gathered = lax.all_gather(normed_two, "mlp", axis=0, tiled=True)
    hidden_pre = jnp.dot(gathered, mlp_in, preferred_element_type=jnp.float32) + mlp_in_bias
    hidden = gelu_tanh(hidden_pre).astype(jnp.bfloat16)
    hidden_rows = hidden
    result = (
        lax.psum_scatter(
            jnp.dot(hidden_rows, mlp_out, preferred_element_type=jnp.float32).astype(jnp.bfloat16),
            "mlp",
            scatter_dimension=0,
            tiled=True,
        ).astype(jnp.float32)
        + mlp_out_bias
    )
    layer_output = (middle + result).astype(jnp.bfloat16)
    upstream = cotangent.astype(jnp.float32)
    d_out_bias = jnp.sum(upstream, axis=0)
    part_rows = lax.all_gather(cotangent, "mlp", axis=0, tiled=True)
    hidden_rows = hidden
    acc_out = jnp.einsum("rf,rd->fd", hidden_rows, part_rows, preferred_element_type=jnp.float32)
    d_hidden = jnp.einsum("rd,fd->rf", part_rows, mlp_out, preferred_element_type=jnp.float32)
    pre_rows = hidden_pre
    d_rows = gelu_backward(pre_rows, d_hidden).astype(jnp.bfloat16)
    d_mlp_out = acc_out
    d_mlp_in_bias = jnp.sum(d_rows, axis=0, dtype=jnp.float32)
    d_mlp_in = jnp.einsum("rd,rf->df", gathered, d_rows, preferred_element_type=jnp.float32)
    pre_rows = d_rows
    d_normed_two = lax.psum_scatter(
        jnp.einsum("rf,df->rd", pre_rows, mlp_in, preferred_element_type=jnp.float32).astype(
            jnp.bfloat16
        ),
        "mlp",
        scatter_dimension=0,
        tiled=True,
    ).astype(jnp.float32)
    d_middle_norm, d_ln2_gain, d_ln2_bias = norm_backward(middle, gain_two, bias_two, d_normed_two)
    d_middle = upstream + d_middle_norm
    d_branch = d_middle.astype(jnp.bfloat16)
    d_attn_out_bias = jnp.sum(d_branch, axis=0, dtype=jnp.float32)
    d_attn_out = jnp.einsum("re,rd->ed", mixture, d_branch, preferred_element_type=jnp.float32)
    d_mixture = jnp.einsum(
        "rd,ed->re", d_branch, attn_out, preferred_element_type=jnp.float32
    ).astype(jnp.bfloat16)
    d_mix_h = d_mixture.reshape(seg_count, L, H, HD)
    reading_low = reading.astype(jnp.bfloat16)
    segment = 0
    allowed = causal & (documents[segment][:, None] == documents[segment][None, :])
    scores = (
        jnp.einsum(
            "qhd,khd->hqk", query_h[segment], key_h[segment], preferred_element_type=jnp.float32
        )
        * score_scale
    )
    scores = jnp.where(allowed[None], scores, -1000000000.0)
    weights = jnp.exp(scores - local_lse[segment])
    d_weights = jnp.einsum(
        "qhd,khd->hqk", d_mix_h[segment], value_h[segment], preferred_element_type=jnp.float32
    )
    row_inner = jnp.sum(weights * d_weights, axis=-1, keepdims=True)
    d_scores = (weights * (d_weights - row_inner)).astype(jnp.bfloat16)
    d_query_f = (
        jnp.einsum("hqk,khd->qhd", d_scores, key_h[segment], preferred_element_type=jnp.float32)
        * score_scale
    )
    d_key_parts = [
        jnp.einsum("hqk,qhd->khd", d_scores, query_h[segment], preferred_element_type=jnp.float32)
        * score_scale
    ]
    d_value_parts = [
        jnp.einsum(
            "hqk,qhd->khd",
            weights.astype(jnp.bfloat16),
            d_mix_h[segment],
            preferred_element_type=jnp.float32,
        )
    ]
    d_remote = d_mix_h[segment] * reading_low[segment][:, None, None]
    mem_scores = (
        jnp.einsum(
            "qhd,khd->hqk", query_h[segment], mem_key_h[segment], preferred_element_type=jnp.float32
        )
        * score_scale
    )
    mem_weights = jnp.exp(mem_scores - memory_lse[segment])
    d_mem_weights = jnp.einsum(
        "qhd,khd->hqk", d_remote, mem_value_h[segment], preferred_element_type=jnp.float32
    )
    mem_inner = jnp.sum(mem_weights * d_mem_weights, axis=-1, keepdims=True)
    d_mem_scores = (mem_weights * (d_mem_weights - mem_inner)).astype(jnp.bfloat16)
    d_query_f = (
        d_query_f
        + jnp.einsum(
            "hqk,khd->qhd", d_mem_scores, mem_key_h[segment], preferred_element_type=jnp.float32
        )
        * score_scale
    )
    d_query_parts = [d_query_f]
    d_mem_key_parts = [
        jnp.einsum(
            "hqk,qhd->khd", d_mem_scores, query_h[segment], preferred_element_type=jnp.float32
        )
        * score_scale
    ]
    d_mem_value_parts = [
        jnp.einsum(
            "hqk,qhd->khd",
            mem_weights.astype(jnp.bfloat16),
            d_remote,
            preferred_element_type=jnp.float32,
        )
    ]
    d_qkv = jnp.concatenate(
        [
            jnp.stack(d_query_parts).reshape(own_rows, D),
            jnp.stack(d_key_parts).reshape(own_rows, D),
            jnp.stack(d_value_parts).reshape(own_rows, D),
        ],
        axis=1,
    ).astype(jnp.bfloat16)
    d_mem_kv = jnp.concatenate(
        [
            jnp.stack(d_mem_key_parts).reshape(seg_count, NB, D),
            jnp.stack(d_mem_value_parts).reshape(seg_count, NB, D),
        ],
        axis=2,
    ).astype(jnp.bfloat16)
    d_kv_weight = jnp.einsum(
        "sjd,sje->de", coefficients, d_mem_kv, preferred_element_type=jnp.float32
    )
    d_coefficients = jnp.einsum(
        "sje,de->sjd", d_mem_kv, attn_in[:, D:], preferred_element_type=jnp.float32
    ).astype(jnp.bfloat16)
    from_following = shifted(d_coefficients[0], "mlp", -1)
    d_summary = jnp.concatenate([d_coefficients[1:], from_following[None]], axis=0).astype(
        jnp.float32
    )
    d_memory_rows = jnp.einsum("sjt,sjd->std", basis, d_summary, precision=highest)
    d_normed = jnp.einsum(
        "rc,dc->rd", d_qkv, attn_in, preferred_element_type=jnp.float32
    ) + d_memory_rows.reshape(own_rows, D)
    d_attn_in = jnp.einsum(
        "rd,rc->dc", normed, d_qkv, preferred_element_type=jnp.float32
    ) + jnp.concatenate([jnp.zeros((D, D), jnp.float32), d_kv_weight], axis=1)
    d_qv_bias = jnp.stack(
        [
            jnp.sum(d_qkv[:, :D], axis=0, dtype=jnp.float32),
            jnp.sum(d_qkv[:, 2 * D :], axis=0, dtype=jnp.float32)
            + jnp.sum(d_mem_kv[:, :, D:], axis=(0, 1), dtype=jnp.float32),
        ]
    )
    d_in_norm, d_ln1_gain, d_ln1_bias = norm_backward(activations, gain_one, bias_one, d_normed)
    input_grad = (d_middle + d_in_norm).astype(jnp.bfloat16)
    (
        d_attn_in,
        d_qv_bias,
        d_attn_out,
        d_attn_out_bias,
        d_ln1_gain,
        d_ln1_bias,
        d_ln2_gain,
        d_ln2_bias,
        d_out_bias,
    ) = lax.psum(
        (
            d_attn_in,
            d_qv_bias,
            d_attn_out,
            d_attn_out_bias,
            d_ln1_gain,
            d_ln1_bias,
            d_ln2_gain,
            d_ln2_bias,
            d_out_bias,
        ),
        ("batch", "mlp"),
    )
    d_mlp_in, d_mlp_in_bias, d_mlp_out = (
        lax.psum(d_mlp_in.astype(jnp.bfloat16), "batch").astype(jnp.float32),
        lax.psum(d_mlp_in_bias.astype(jnp.bfloat16), "batch").astype(jnp.float32),
        lax.psum(d_mlp_out.astype(jnp.bfloat16), "batch").astype(jnp.float32),
    )
    return (
        layer_output,
        input_grad,
        d_ln1_gain,
        d_ln1_bias,
        d_attn_in,
        d_qv_bias,
        d_attn_out,
        d_attn_out_bias,
        d_ln2_gain,
        d_ln2_bias,
        d_mlp_in,
        d_mlp_in_bias,
        d_mlp_out,
        d_out_bias,
    )


def solution(mesh):
    placed = (
        P(("batch", "mlp"), None),
        P(("batch", "mlp"), None),
        P(),
        P(),
        P(),
        P(),
        P(),
        P(),
        P(),
        P(),
        P(None, "mlp"),
        P("mlp"),
        P("mlp", None),
        P(),
        P(("batch", "mlp"), None),
    )
    return jax.shard_map(
        shards,
        mesh=mesh,
        in_specs=placed,
        out_specs=(
            P(("batch", "mlp"), None),
            P(("batch", "mlp"), None),
            P(),
            P(),
            P(),
            P(),
            P(),
            P(),
            P(),
            P(),
            P(None, "mlp"),
            P("mlp"),
            P("mlp", None),
            P(),
        ),
        check_vma=False,
    )
```

profile of v0, /device:TPU:0, one launch (start us, length us, event | category | flops | bytes accessed | tf_op | source)
XLA Modules:
  0.0 547.2 jit_solution(7533551141080373832)
XLA Ops:
  14.0 4.1 convolution_convert_fusion.5
  18.1 5.8 %collective-permute-start = (bf16[512,768]{1,0:T(8,128)(2,1)}, bf16[512,768]{1,0:T(8,128)(2,1)}, u32[]{:S(2)}, u32[]{:S(2)}) collective-permute-start(bf16[512,768]{1,0:T(8,128)(2,1)} %convolution_convert_fusion.5), channel_id=1, source_target_pairs={{0,1},{2,3},{4,5},{6,7},{8,9},{10,11},{12,13},{14,15},{16,17},{18,... | collective-permute-start | bytes 2359304 | tf_op jit(solution)/shard_map/ppermute | solution.py:20
  23.9 2.2 fusion.101
  29.9 2.3 copy.68
  32.8 2.3 copy.66
  35.1 3.2 fusion.21
  38.3 2.6 fusion
  40.9 1.9 copy-done.3
  42.8 6.1 %fusion.19 = f32[12,64,512]{2,1,0:T(8,128)} fusion(bf16[512,12,64]{0,2,1:T(8,128)(2,1)} %bitcast.90, f32[12,512]{1,0:T(8,128)S(1)} %fusion, f32[12,512]{1,0:T(8,128)S(1)} %get-tuple-element.47, f32[12,512,512]{1,2,0:T(8,128)S(1)} %get-tuple-element.48, pred[512,512]{0,1:T(8,128)(4,1)S(1)} %fusion.58), kind=kOutput, calls=%fused_computation.34 | convolution fusion | flops 418381824 | bytes 15253504 | tf_op jit(solution)/shard_map/hqk,khd->qhd/dot_general | solution.py:133
  50.7 3.3 convolution_bitcast_fusion
  56.1 2.3 copy.71
  58.4 7.5 %multiply_reduce_fusion.2 = (f32[12,512]{1,0:T(8,128)S(1)}, f32[12,512,512]{1,2,0:T(8,128)}) fusion(bf16[512,12,64]{0,2,1:T(8,128)(2,1)S(1)} %bitcast.79, bf16[512,12,64]{0,2,1:T(8,128)(2,1)} %bitcast.88), kind=kOutput, calls=%fused_computation.13 | convolution fusion | flops 408938496 | bytes 14180352 | tf_op jit(solution)/shard_map/qhd,khd->hqk/dot_general | solution.py:140
  65.8 2.3 copy.70
  68.2 6.8 %fusion.1 = f32[12,512]{1,0:T(8,128)S(1)} fusion(f32[12,512,512]{1,2,0:T(8,128)} %get-tuple-element.50, f32[12,512]{1,0:T(8,128)S(1)} %get-tuple-element.49), kind=kLoop, calls=%fused_computation.12 | loop fusion | flops 9431040 | bytes 12632064 | tf_op jit(solution)/shard_map/reduce_sum | solution.py:48
  76.3 4.5 add_convert_fusion.3
  85.1 26.8 %all-gather.3.cloned.1.call-done = bf16[1024,768]{1,0:T(8,128)(2,1)} async-done(((bf16[512,768]{1,0:T(8,128)(2,1)}), bf16[1024,768]{1,0:T(8,128)(2,1)}) %all-gather.3.cloned.1.call-update) | async-done | bytes 1572880 | tf_op jit(solution)/shard_map/all_gather | solution.py:159
  111.9 7.5 %fusion.112 = f32[1024,1536]{1,0:T(8,128)} fusion(bf16[1024,768]{1,0:T(8,128)(2,1)} %all-gather.3.cloned.1.call-done, bf16[768,1536]{1,0:T(8,128)(2,1)} %param.25), kind=kOutput, calls=%fused_computation.171 | convolution fusion | flops 2415919104 | bytes 10223616 | tf_op jit(solution)/shard_map/dot_general | solution.py:160
  119.3 21.3 %all-gather.5.cloned.1.call-done = bf16[1024,768]{1,0:T(8,128)(2,1)} async-done(((bf16[512,768]{1,0:T(8,128)(2,1)}), bf16[1024,768]{1,0:T(8,128)(2,1)}) %all-gather.5.cloned.1.call-update) | async-done | bytes 1572880 | tf_op jit(solution)/shard_map/all_gather | solution.py:175
  140.7 10.7 %fusion.106 = (bf16[1536]{0:T(1024)(128)(2,1)}, bf16[1024,1536]{1,0:T(8,128)(2,1)S(1)}) fusion(f32[1024,1536]{1,0:T(8,128)} %fusion.112, f32[1536]{0:T(1024)S(1)} %convert_element_type.229, bf16[1024,768]{1,0:T(8,128)(2,1)} %all-gather.5.cloned.1.call-done, bf16[1536,768]{1,0:T(8,128)(2,1)S(1)} %copy-done), kind=kOutput, calls=%fused_computation.167 | convolution fusion | flops 2456812032 | bytes 13378560 | tf_op jit(solution)/shard_map/rd,fd->rf/dot_general | solution.py:178
  153.0 3.7 convolution_convert_fusion.2
  156.8 7.9 %convolution_convert_fusion.3 = bf16[1024,768]{1,0:T(8,128)(2,1)} fusion(bf16[1536,768]{1,0:T(8,128)(2,1)S(1)} %copy-done, f32[1024,1536]{1,0:T(8,128)} %fusion.112, f32[1536]{0:T(1024)S(1)} %convert_element_type.229), kind=kOutput, calls=%fused_computation.63 | convolution fusion | flops 2432434176 | bytes 10229760 | tf_op jit(solution)/shard_map/dot_general | solution.py:165
  166.4 6.5 %convolution_convert_fusion.1 = bf16[768,1536]{1,0:T(8,128)(2,1)} fusion(bf16[1024,768]{1,0:T(8,128)(2,1)} %all-gather.3.cloned.1.call-done, bf16[1024,1536]{1,0:T(8,128)(2,1)} %copy-done.67), kind=kOutput, calls=%fused_computation.38 | convolution fusion | flops 2417098752 | bytes 7077888 | tf_op jit(solution)/shard_map/rd,rf->df/dot_general | solution.py:183
  173.0 8.2 %convolution_convert_fusion = bf16[1536,768]{1,0:T(8,128)(2,1)} fusion(bf16[1024,768]{1,0:T(8,128)(2,1)S(1)} %copy-done.64, f32[1024,1536]{1,0:T(8,128)} %fusion.112, f32[1536]{0:T(1024)S(1)} %copy-done.45), kind=kOutput, calls=%fused_computation.37 | convolution fusion | flops 2432827392 | bytes 10229760 | tf_op jit(solution)/shard_map/rf,rd->fd/dot_general | solution.py:177
  181.3 1.8 reduce-scatter.5.cloned.1.call-done
  184.9 26.5 %reduce-scatter.3.cloned.1.call-done = bf16[512,768]{1,0:T(8,128)(2,1)} async-done(((bf16[1024,768]{1,0:T(8,128)(2,1)}), bf16[512,768]{1,0:T(8,128)(2,1)}) %reduce-scatter.3.cloned.1.call-update) | async-done | bytes 786448 | tf_op jit(solution)/shard_map/reduce_scatter | solution.py:164
  211.4 3.1 fusion.109
  218.0 11.0 %multiply_reduce_fusion = (f32[12,512]{1,0:T(8,128)S(1)}, f32[12,512,512]{1,2,0:T(8,128)}) fusion(f32[12,512,512]{1,2,0:T(8,128)} %get-tuple-element.50, f32[12,512]{1,0:T(8,128)S(1)} %log_add_fusion, bf16[512,12,64]{0,2,1:T(8,128)(2,1)S(1)} %bitcast.99, bf16[512,12,64]{0,2,1:T(8,128)(2,1)S(1)} %bitcast.82, bf16[512]{0:T(512)(128)(2,1)S(1)} %copy-done.43), kind=kOutput, calls=%fused_computation.1 | convolution fusion | flops 415623168 | bytes 26788864 | tf_op jit(solution)/shard_map/qhd,khd->hqk/dot_general | solution.py:242
  229.0 7.3 %convert_reduce_fusion.3 = (f32[12,64]{1,0:T(8,128)S(1)}, bf16[12,64,512]{2,1,0:T(8,128)(2,1)S(1)}) fusion(f32[12,512,512]{1,2,0:T(8,128)} %get-tuple-element.50, f32[12,512]{1,0:T(8,128)S(1)} %log_add_fusion, bf16[512,12,64]{0,2,1:T(8,128)(2,1)S(1)} %bitcast.83, bf16[512]{0:T(512)(128)(2,1)S(1)} %copy-done.43), kind=kOutput, calls=%fused_computation.80 | convolution fusion | flops 413662464 | bytes 14184448 | tf_op jit(solution)/shard_map/hqk,qhd->khd/dot_general | solution.py:262
  236.3 6.8 %multiply_reduce_fusion.1 = (f32[12,512]{1,0:T(8,128)S(1)}, f32[12,512,512]{1,2,0:T(8,128)}) fusion(f32[12,512]{1,0:T(8,128)S(1)} %log_add_fusion.1, f32[12,512,512]{1,2,0:T(8,128)S(1)} %bitcast.75, pred[512,512]{0,1:T(8,128)(4,1)S(1)} %fusion.58, bf16[512,12,64]{0,2,1:T(8,128)(2,1)S(1)} %bitcast.84, bf16[512,12,64]{0,2,1:T(8,128)(2,1)S(1)} %bitcast.91), kind=kOutput, calls=%fused_computation.4 | convolution fusion | flops 418375680 | bytes 27049984 | tf_op jit(solution)/shard_map/qhd,khd->hqk/dot_general | solution.py:213
  243.2 11.0 %multiply_convert_fusion.1 = bf16[12,512,512]{1,2,0:T(8,128)(2,1)} fusion(f32[12,512,512]{1,2,0:T(8,128)} %get-tuple-element.54, f32[12,512]{1,0:T(8,128)S(1)} %get-tuple-element.53, f32[12,512]{1,0:T(8,128)S(1)} %log_add_fusion.1, f32[12,512,512]{1,2,0:T(8,128)S(1)} %bitcast.75, pred[512,512]{0,1:T(8,128)(4,1)S(1)} %fusion.58), kind=kLoop, calls=%fused_computation.3 | loop fusion | flops 18874368 | bytes 31768576 | tf_op jit(solution)/shard_map/convert_element_type | solution.py:217
  254.2 4.1 fusion.113
  258.3 5.8 %multiply_convert_fusion.3 = bf16[12,64,512]{2,1,0:T(8,128)(2,1)} fusion(bf16[512,12,64]{0,2,1:T(8,128)(2,1)S(1)} %bitcast.80, bf16[12,512,512]{1,2,0:T(8,128)(2,1)} %multiply_convert_fusion.1), kind=kOutput, calls=%fused_computation.86 | convolution fusion | flops 403439616 | bytes 7864320 | tf_op jit(solution)/shard_map/hqk,qhd->khd/dot_general | solution.py:223
  264.2 10.2 %multiply_convert_fusion = bf16[12,512,512]{1,2,0:T(8,128)(2,1)} fusion(f32[12,512,512]{1,2,0:T(8,128)} %get-tuple-element.56, f32[12,512,512]{1,2,0:T(8,128)S(1)} %bitcast.73, f32[12,512]{1,0:T(8,128)S(1)} %get-tuple-element.55, f32[12,512]{1,0:T(8,128)S(1)} %log_add_fusion), kind=kLoop, calls=%fused_computation | loop fusion | flops 15728640 | bytes 31506432 | tf_op jit(solution)/shard_map/convert_element_type | solution.py:246
  274.4 4.9 multiply_convert_fusion.2
  279.4 2.2 fusion.114
  281.6 2.9 fusion.59
  285.7 3.2 fusion.46
  289.0 7.1 %pad_add_fusion = f32[768,2304]{1,0:T(8,128)} fusion(f32[768,1536]{1,0:T(8,128)S(1)} %fusion.59, bf16[512,768]{0,1:T(8,128)(2,1)S(1)} %bitcast.100, bf16[512,768]{0,1:T(8,128)(2,1)S(1)} %bitcast.104, bf16[512,768]{0,1:T(8,128)(2,1)S(1)} %bitcast.94, bf16[512,768]{1,0:T(8,128)(2,1)S(1)} %copy-done.10, f32[768]{0:T(1024)S(1)} %copy-done.48, ...), kind=kOutput, calls=%fused_computation.20 | convolution fusion | flops 1823145984 | bytes 14952448 | tf_op jit(solution)/shard_map/rd,rc->dc/dot_general | solution.py:298
  296.8 34.8 %psum.93 = bf16[1536]{0:T(1024)(128)(2,1)S(1)} all-reduce(bf16[1536]{0:T(1024)(128)(2,1)S(1)} %copy-done.49), channel_id=1, replica_groups=mesh['batch'=16,'mlp'=2] {'batch'}, use_global_device_ids=true, to_apply=%region_37.38 | all-reduce | flops 1536 | bytes 6144 | tf_op jit(solution)/shard_map/psum | solution.py:336
  332.6 4.6 convert_element_type.253
  337.3 2.5 convert_element_type.256
  341.3 3.2 fusion.43
  346.3 2.1 fusion.62
  348.4 33.7 %collective-permute-done.1 = bf16[512,768]{1,0:T(8,128)(2,1)S(1)} collective-permute-done((bf16[512,768]{1,0:T(8,128)(2,1)S(1)}, bf16[512,768]{1,0:T(8,128)(2,1)S(1)}, u32[]{:S(2)}, u32[]{:S(2)}) %collective-permute-start.1) | collective-permute-done | bytes 786464 | tf_op jit(solution)/shard_map/ppermute | solution.py:20
  382.1 2.2 fusion.105
  387.4 41.2 %all-reduce.1 = (f32[768]{0:T(1024)}, f32[768]{0:T(1024)}, f32[2,768]{1,0:T(2,128)}, f32[768]{0:T(1024)}, f32[768]{0:T(1024)}, /*index=5*/f32[768]{0:T(1024)}, f32[768]{0:T(1024)}) all-reduce(f32[768]{0:T(1024)S(1)} %get-tuple-element.14, f32[768]{0:T(1024)S(1)} %get-tuple-element.18, ...), channel_id=1, replica_groups=mesh['batch'=16,'mlp'=2] {'batch','mlp'}, use_global_device_ids=true, to_apply=%region_20.21 | all-reduce | flops 6144 | bytes 49152 | tf_op jit(solution)/shard_map/psum | solution.py:320
  428.7 103.5 %all-reduce.7.cloned.1.call-done = (f32[768,2304]{1,0:T(8,128)}, f32[768,768]{1,0:T(8,128)}) async-done(((f32[768,2304]{1,0:T(8,128)}, f32[768,768]{1,0:T(8,128)}), (f32[768,2304]{1,0:T(8,128)}, f32[768,768]{1,0:T(8,128)})) %all-reduce.7.cloned.1.call-update) | async-done | bytes 9437200 | tf_op jit(solution)/shard_map/psum | solution.py:320
  532.2 6.6 %copy.92 = f32[768,2304]{1,0:T(8,128)} copy(f32[768,2304]{1,0:T(8,128)} %get-tuple-element.68) | data formatting | bytes 14155776
  (226 shorter events, 39.2 us)
Async XLA Ops:
  7.2 133.5 %copy-start = (bf16[1536,768]{1,0:T(8,128)(2,1)S(1)}, bf16[1536,768]{1,0:T(8,128)(2,1)}, u32[]{:S(2)}) copy-start(bf16[1536,768]{1,0:T(8,128)(2,1)} %param.27) | copy-start | bytes 7077892
  7.2 104.7 %all-gather.3.cloned.1.call-start = ((), (), s32[]{:S(2)}) async-start(), calls=%async_computation.2 | async-start | bytes 2359296 | tf_op jit(solution)/shard_map/all_gather | solution.py:159
  9.3 8.8 %copy-start.54 = (f32[512]{0:T(512)}, f32[512]{0:T(512)S(1)}, u32[]{:S(2)}) copy-start(f32[512]{0:T(512)S(1)} %compare_convert_fusion.1) | copy-start | bytes 6148
  9.4 8.7 %copy-start.58 = (f32[512]{0:T(512)}, f32[512]{0:T(512)S(1)}, u32[]{:S(2)}) copy-start(f32[512]{0:T(512)S(1)} %get-tuple-element.61) | copy-start | bytes 6148
  10.7 13.2 %copy-start.34 = (f32[512]{0:T(512)}, f32[512]{0:T(512)S(1)}, u32[]{:S(2)}) copy-start(f32[512]{0:T(512)S(1)} %broadcast_multiply_fusion.1) | copy-start | bytes 6148
  12.2 11.7 %copy-start.36 = (f32[512]{0:T(512)}, f32[512]{0:T(512)S(1)}, u32[]{:S(2)}) copy-start(f32[512]{0:T(512)S(1)} %fusion.83) | copy-start | bytes 6148
  12.9 11.0 %copy-start.32 = (f32[768]{0:T(1024)}, f32[768]{0:T(1024)S(1)}, u32[]{:S(2)}) copy-start(f32[768]{0:T(1024)S(1)} %convert_element_type.209) | copy-start | bytes 9220
  13.6 10.3 %copy-start.47 = (f32[768]{0:T(1024)}, f32[768]{0:T(1024)S(1)}, u32[]{:S(2)}) copy-start(f32[768]{0:T(1024)S(1)} %convert_element_type.210) | copy-start | bytes 9220
  14.0 9.9 %copy-start.8 = (bf16[512,768]{1,0:T(8,128)(2,1)S(1)}, bf16[512,768]{1,0:T(8,128)(2,1)}, u32[]{:S(2)}) copy-start(bf16[512,768]{1,0:T(8,128)(2,1)} %param.15) | copy-start | bytes 2359300
  14.0 9.9 %copy-start.61 = (bf16[768,2304]{1,0:T(8,128)(2,1)S(1)}, bf16[768,2304]{1,0:T(8,128)(2,1)}, u32[]{:S(2)}) copy-start(bf16[768,2304]{1,0:T(8,128)(2,1)} %param.19) | copy-start | bytes 10616836
  18.1 8.0 %copy-start.42 = (bf16[2,768]{1,0:T(2,128)(2,1)S(1)}, bf16[2,768]{1,0:T(2,128)(2,1)}, u32[]{:S(2)}) copy-start(bf16[2,768]{1,0:T(2,128)(2,1)} %param.20) | copy-start | bytes 9220
  18.1 32.6 %collective-permute-start = (bf16[512,768]{1,0:T(8,128)(2,1)}, bf16[512,768]{1,0:T(8,128)(2,1)}, u32[]{:S(2)}, u32[]{:S(2)}) collective-permute-start(bf16[512,768]{1,0:T(8,128)(2,1)} %convolution_convert_fusion.5), channel_id=1, source_target_pairs={{0,1},{2,3},{4,5},{6,7},{8,9},{10,11},{12,13},{14,15},{16,17},{18,... | collective-permute-start | bytes 2359304 | tf_op jit(solution)/shard_map/ppermute | solution.py:20
  42.8 6.1 %copy-start.50 = (bf16[768]{0:T(1024)(128)(2,1)S(1)}, bf16[768]{0:T(1024)(128)(2,1)}, u32[]{:S(2)}) copy-start(bf16[768]{0:T(1024)(128)(2,1)} %param.22) | copy-start | bytes 4612
  42.8 6.1 %copy-start.51 = (bf16[768]{0:T(1024)(128)(2,1)S(1)}, bf16[768]{0:T(1024)(128)(2,1)}, u32[]{:S(2)}) copy-start(bf16[768]{0:T(1024)(128)(2,1)} %param.23) | copy-start | bytes 4612
  42.8 6.1 %copy-start.52 = (bf16[768]{0:T(1024)(128)(2,1)S(1)}, bf16[768]{0:T(1024)(128)(2,1)}, u32[]{:S(2)}) copy-start(bf16[768]{0:T(1024)(128)(2,1)} %param.24) | copy-start | bytes 4612
  68.2 8.2 %copy-start.2 = (f32[12,512,512]{1,2,0:T(8,128)S(1)}, f32[12,512,512]{1,2,0:T(8,128)}, u32[]{:S(2)}) copy-start(f32[12,512,512]{1,2,0:T(8,128)} %get-tuple-element.50) | copy-start | bytes 37748740
  84.3 56.4 %all-gather.5.cloned.1.call-start = ((), (), s32[]{:S(2)}) async-start(), calls=%async_computation.4 | async-start | bytes 2359296 | tf_op jit(solution)/shard_map/all_gather | solution.py:175
  85.0 98.1 %reduce-scatter.5.cloned.1.call-start = ((), (), s32[]{:S(2)}) async-start(), calls=%async_computation.5 | async-start | bytes 2359296 | tf_op jit(solution)/shard_map/reduce_scatter | solution.py:185
  85.1 71.7 %copy-start.44 = (f32[1536]{0:T(1024)}, f32[1536]{0:T(1024)S(1)}, u32[]{:S(2)}) copy-start(f32[1536]{0:T(1024)S(1)} %convert_element_type.229) | copy-start | bytes 18436
  140.7 12.4 %copy-start.63 = (bf16[768,1536]{1,0:T(8,128)(2,1)S(1)}, bf16[768,1536]{1,0:T(8,128)(2,1)}, u32[]{:S(2)}) copy-start(bf16[768,1536]{1,0:T(8,128)(2,1)} %param.25) | copy-start | bytes 7077892
  156.8 8.3 %copy-start.53 = (bf16[768]{0:T(1024)(128)(2,1)S(1)}, bf16[768]{0:T(1024)(128)(2,1)}, u32[]{:S(2)}) copy-start(bf16[768]{0:T(1024)(128)(2,1)} %param.28) | copy-start | bytes 4612
  156.8 54.6 %reduce-scatter.3.cloned.1.call-start = ((), (), s32[]{:S(2)}) async-start(), calls=%async_computation.3 | async-start | bytes 2359296 | tf_op jit(solution)/shard_map/reduce_scatter | solution.py:164
  164.7 167.9 %all-reduce.9.cloned.1.call-start = ((), (), s32[]{:S(2)}) async-start(), calls=%async_computation.7 | async-start | bytes 9437184 | tf_op jit(solution)/shard_map/psum | solution.py:335
  166.4 6.6 %copy-start.45 = (f32[1536]{0:T(1024)S(1)}, f32[1536]{0:T(1024)}, u32[]{:S(2)}) copy-start(f32[1536]{0:T(1024)} %copy-done.44) | copy-start | bytes 18436
  166.4 6.5 %copy-start.64 = (bf16[1024,768]{1,0:T(8,128)(2,1)S(1)}, bf16[1024,768]{1,0:T(8,128)(2,1)}, u32[]{:S(2)}) copy-start(bf16[1024,768]{1,0:T(8,128)(2,1)} %all-gather.5.cloned.1.call-done) | copy-start | bytes 4718596
  181.2 30.2 %copy-start.41 = (f32[768]{0:T(1024)S(1)}, f32[768]{0:T(1024)}, u32[]{:S(2)}) copy-start(f32[768]{0:T(1024)} %convert_element_type.233) | copy-start | bytes 9220
  181.2 351.0 %all-reduce.7.cloned.1.call-start = ((), (), s32[]{:S(2)}) async-start(), calls=%async_computation.6 | async-start | bytes 18874368 | tf_op jit(solution)/shard_map/psum | solution.py:320
  184.9 30.8 %copy-start.13 = (bf16[512,768]{1,0:T(8,128)(2,1)S(1)}, bf16[512,768]{1,0:T(8,128)(2,1)}, u32[]{:S(2)}) copy-start(bf16[512,768]{1,0:T(8,128)(2,1)} %param.29) | copy-start | bytes 2359300
  218.0 18.3 %slice-start.3 = ((s8[12582912]{0:T(1024)(128)(4,1)}), s8[4194304]{0:T(1024)(128)(4,1)S(1)}, s32[]{:S(2)}) async-start(s8[12582912]{0:T(1024)(128)(4,1)} %bitcast.74), calls=%async_computation.11 | async-start | bytes 8388608
  218.0 18.3 %slice-start.4 = ((s8[12582912]{0:T(1024)(128)(4,1)}), s8[4194304]{0:T(1024)(128)(4,1)S(1)}, s32[]{:S(2)}) async-start(s8[12582912]{0:T(1024)(128)(4,1)} %bitcast.74), calls=%async_computation.12 | async-start | bytes 8388608
  229.0 7.3 %slice-start.5 = ((s8[12582912]{0:T(1024)(128)(4,1)}), s8[4194304]{0:T(1024)(128)(4,1)S(1)}, s32[]{:S(2)}) async-start(s8[12582912]{0:T(1024)(128)(4,1)} %bitcast.74), calls=%async_computation.13 | async-start | bytes 8388608
  229.0 7.3 %copy-start.15 = (bf16[512,768]{0,1:T(8,128)(2,1)S(1)}, bf16[512,768]{0,1:T(8,128)(2,1)}, u32[]{:S(2)}) copy-start(bf16[512,768]{0,1:T(8,128)(2,1)} %copy.66) | copy-start | bytes 2359300
  236.3 45.2 %copy-start.16 = (bf16[12,64,512]{2,1,0:T(8,128)(2,1)}, bf16[12,64,512]{2,1,0:T(8,128)(2,1)S(1)}, u32[]{:S(2)}) copy-start(bf16[12,64,512]{2,1,0:T(8,128)(2,1)S(1)} %get-tuple-element.59) | copy-start | bytes 2359300
  243.2 11.0 %copy-start.11 = (bf16[512,768]{0,1:T(8,128)(2,1)S(1)}, bf16[512,768]{0,1:T(8,128)(2,1)}, u32[]{:S(2)}) copy-start(bf16[512,768]{0,1:T(8,128)(2,1)} %copy.68) | copy-start | bytes 2359300
  243.2 21.0 %slice-start = ((s8[12582912]{0:T(1024)(128)(4,1)}), s8[4194304]{0:T(1024)(128)(4,1)S(1)}, s32[]{:S(2)}) async-start(s8[12582912]{0:T(1024)(128)(4,1)} %bitcast.72), calls=%async_computation.8 | async-start | bytes 8388608
  243.2 21.0 %slice-start.1 = ((s8[12582912]{0:T(1024)(128)(4,1)}), s8[4194304]{0:T(1024)(128)(4,1)S(1)}, s32[]{:S(2)}) async-start(s8[12582912]{0:T(1024)(128)(4,1)} %bitcast.72), calls=%async_computation.9 | async-start | bytes 8388608
  254.2 10.0 %slice-start.2 = ((s8[12582912]{0:T(1024)(128)(4,1)}), s8[4194304]{0:T(1024)(128)(4,1)S(1)}, s32[]{:S(2)}) async-start(s8[12582912]{0:T(1024)(128)(4,1)} %bitcast.72), calls=%async_computation.10 | async-start | bytes 8388608
  274.4 10.1 %slice-start.6 = ((s8[6291456]{0:T(1024)(128)(4,1)}), s8[2097152]{0:T(1024)(128)(4,1)S(1)}, s32[]{:S(2)}) async-start(s8[6291456]{0:T(1024)(128)(4,1)} %bitcast.76), calls=%async_computation.14 | async-start | bytes 4194304
  289.0 7.1 %copy-start.25 = (bf16[12,64,512]{2,1,0:T(8,128)(2,1)}, bf16[12,64,512]{2,1,0:T(8,128)(2,1)S(1)}, u32[]{:S(2)}) copy-start(bf16[12,64,512]{2,1,0:T(8,128)(2,1)S(1)} %fusion.46) | copy-start | bytes 2359300
  344.5 37.5 %collective-permute-start.1 = (bf16[512,768]{1,0:T(8,128)(2,1)S(1)}, bf16[512,768]{1,0:T(8,128)(2,1)S(1)}, u32[]{:S(2)}, u32[]{:S(2)}) collective-permute-start(bf16[512,768]{1,0:T(8,128)(2,1)S(1)} %fusion.43), channel_id=1, source_target_pairs={{1,0},{3,2},{5,4},{7,6},{9,8},{11,10},{13,12},{15,14},{17,16},{19,... | collective-permute-start | bytes 2359304 | tf_op jit(solution)/shard_map/ppermute | solution.py:20
  346.3 35.8 %copy-start.55 = (f32[512]{0:T(512)S(1)}, f32[512]{0:T(512)}, u32[]{:S(2)}) copy-start(f32[512]{0:T(512)} %copy-done.54) | copy-start | bytes 6148
  346.3 35.8 %copy-start.57 = (f32[512]{0:T(512)S(1)}, f32[512]{0:T(512)}, u32[]{:S(2)}) copy-start(f32[512]{0:T(512)} %copy-done.56) | copy-start | bytes 6148
  346.3 35.8 %copy-start.59 = (f32[512]{0:T(512)S(1)}, f32[512]{0:T(512)}, u32[]{:S(2)}) copy-start(f32[512]{0:T(512)} %copy-done.58) | copy-start | bytes 6148
  346.3 35.8 %copy-start.69 = (f32[512]{0:T(512)S(1)}, f32[512]{0:T(512)}, u32[]{:S(2)}) copy-start(f32[512]{0:T(512)} %copy-done.68) | copy-start | bytes 6148
  348.4 35.9 %copy-start.39 = (f32[512]{0:T(512)S(1)}, f32[512]{0:T(512)}, u32[]{:S(2)}) copy-start(f32[512]{0:T(512)} %copy-done.38) | copy-start | bytes 6148
  348.4 36.8 %copy-start.14 = (bf16[512,768]{1,0:T(8,128)(2,1)S(1)}, bf16[512,768]{1,0:T(8,128)(2,1)}, u32[]{:S(2)}) copy-start(bf16[512,768]{1,0:T(8,128)(2,1)} %param.29) | copy-start | bytes 2359300
  532.2 6.6 %copy-start.24 = (f32[768,768]{1,0:T(8,128)S(1)}, f32[768,768]{1,0:T(8,128)}, u32[]{:S(2)}) copy-start(f32[768,768]{1,0:T(8,128)} %get-tuple-element.70) | copy-start | bytes 7077892
  532.2 8.0 %copy-start.1 = (bf16[1536,768]{1,0:T(8,128)(2,1)S(1)}, bf16[1536,768]{1,0:T(8,128)(2,1)}, u32[]{:S(2)}) copy-start(bf16[1536,768]{1,0:T(8,128)(2,1)} %param.27) | copy-start | bytes 7077892
  (38 other events, 130.4 us)
Sparse Core Ops, SparseCore 0:
  84.4 27.4 all-gather.2
  113.4 27.1 all-gather.4
  156.9 26.1 reduce-scatter.4
  185.2 26.1 reduce-scatter.2
  215.5 117.1 all-reduce.8
  339.0 193.1 all-reduce.6
where the time goes:
time: 556 us; the launch traced here: 547 us
  waiting for transfers between devices  215 us (39%)
  matrix products  141 us (25%)
  blocking collectives  76 us (14%)
  other arithmetic  59.9 us (11%)
  local copies, waits for them, and re-layouts  31.8 us (6%)
  between operations  16 us (3%)
  starting transfers between devices  7.71 us (1%)
    psum x1, waiting for transfers between devices, shards(): lax.psum((d_attn_in, d_qv_bias, d_attn_out, d_attn_out_bias, d_ln1_gain,...  104 us
    psum x1, blocking collectives, shards(): lax.psum((d_attn_in, d_qv_bias, d_attn_out, d_attn_out_bias, d_ln1_gain,...  41.2 us
    psum x1, blocking collectives, shards(): lax.psum(d_mlp_in_bias.astype(jnp.bfloat16), 'batch').astype(jnp.float32)  34.8 us
    ppermute x2, waiting for transfers between devices, shifted(): return lax.ppermute(value, axis, pairs)  33.7 us
    all_gather x1, waiting for transfers between devices, shards(): gathered = lax.all_gather(normed_two, 'mlp', axis=0, tiled=True)  26.8 us
    reduce_scatter x1, waiting for transfers between devices, shards(): lax.psum_scatter(jnp.dot(hidden_rows, mlp_out, preferred_element_type=jnp...  26.5 us
    all_gather x1, waiting for transfers between devices, shards(): part_rows = lax.all_gather(cotangent, 'mlp', axis=0, tiled=True)  21.3 us
    unnamed x158, local copies, waits for them, and re-layouts  17.5 us
  transfers between devices with their start and end apart: 8, of which 7 were waited for; matrix products, arithmetic and copies ran while one was open for 29% of the time, Pallas kernels for 0%

commit v1 on v0

v1 whole, which is shorter than its diff:
```python
import functools

import jax
import jax.numpy as jnp
from jax import lax
from jax.experimental import pallas as pl
from jax.experimental.pallas import tpu as pltpu
from jax.sharding import PartitionSpec as P

D = 768
H = 12
HD = 64
NB = 512
L = 512
NDOC = 3
HALF = L // 2
PAIRS = H // 2
LANES = 2 * HD

LOG2E = 1.4426950408889634
SCORE_LOG2 = LOG2E * HD**-0.5
MASKED = -1e30

bf16 = jnp.bfloat16
f32 = jnp.float32


def dot(a, b):
    return jnp.dot(a, b, preferred_element_type=f32)


def dot_nt(a, b):
    return lax.dot_general(a, b, (((1,), (1,)), ((), ())), preferred_element_type=f32)


def layer_norm(matrix, gain_row, shift_row):
    center = jnp.mean(matrix, axis=-1, keepdims=True)
    centered = matrix - center
    spread = jnp.mean(centered * centered, axis=-1, keepdims=True)
    return centered * lax.rsqrt(spread + 1e-05) * gain_row + shift_row


def norm_backward(matrix, gain_row, shift_row, upstream):
    unused, pullback = jax.vjp(layer_norm, matrix, gain_row, shift_row)
    return pullback(upstream)


def head_lanes(matrix, head):
    lane = lax.broadcasted_iota(jnp.int32, (1, LANES), 1)
    return jnp.where(lane // HD == head, matrix, jnp.zeros_like(matrix))


def fill_mask(lens, mask):
    key = lax.broadcasted_iota(jnp.int32, (L, L), 0)
    query = lax.broadcasted_iota(jnp.int32, (L, L), 1)
    one = lens[0, 0]
    two = one + lens[0, 1]
    start = jnp.where(query >= two, two, jnp.where(query >= one, one, 0))
    mask[...] = jnp.where((key <= query) & (key >= start), 0.0, MASKED)


def local_kernel(lens, q_ref, k_ref, v_ref, out_ref, lse_ref, mask, turned):
    @pl.when(pl.program_id(0) == 0)
    def _():
        fill_mask(lens, mask)

    q, k = q_ref[...], k_ref[...]
    v_t = v_ref[...].T
    for head in range(2):
        q_head = head_lanes(q, head)
        rows = slice(head * HD, (head + 1) * HD)
        for part in range(2):
            keys = HALF * (part + 1)
            cols = slice(part * HALF, (part + 1) * HALF)
            s = dot_nt(k[:keys], q_head[cols]) * SCORE_LOG2 + mask[:keys, cols]
            top = jnp.max(s, axis=0, keepdims=True)
            e = jnp.exp2(s - top)
            total = jnp.sum(e, axis=0, keepdims=True)
            out = dot(v_t[rows, :keys], e.astype(bf16))
            turned[rows, cols] = out / total
            lse_ref[0, head : head + 1, cols] = top + jnp.log2(total)
    out_ref[...] = turned[...].T


def local_attention(lens, qkv):
    column = lambda k: pl.BlockSpec((L, LANES), lambda i: (0, k * PAIRS + i))
    return pl.pallas_call(
        local_kernel,
        grid=(PAIRS,),
        in_specs=[pl.BlockSpec(memory_space=pltpu.SMEM), column(0), column(1), column(2)],
        out_specs=[column(0), pl.BlockSpec((1, 8, L), lambda i: (i, 0, 0))],
        out_shape=[
            jax.ShapeDtypeStruct((L, D), f32),
            jax.ShapeDtypeStruct((PAIRS, 8, L), f32),
        ],
        scratch_shapes=[pltpu.VMEM((L, L), f32), pltpu.VMEM((LANES, L), f32)],
        cost_estimate=pl.CostEstimate(
            flops=H * 12 * HALF * HALF * 256, bytes_accessed=8 * L * D, transcendentals=H * L * L
        ),
        name="local_attention",
    )(lens, qkv, qkv, qkv)


def basis_rows(last_len, transposed):
    shape = (HALF, NB) if transposed else (NB, HALF)
    slot_dim, place_dim = (1, 0) if transposed else (0, 1)
    slot = lax.broadcasted_iota(jnp.int32, shape, slot_dim).astype(f32)
    place = lax.broadcasted_iota(jnp.int32, shape, place_dim).astype(f32)
    offsets = place - HALF + last_len + 0.5
    distances = (slot + 0.5) / NB * last_len - offsets
    weights = jnp.where(offsets > 0.0, jnp.exp(-0.5 * distances * distances), 0.0)
    return weights / jnp.sum(weights, axis=place_dim, keepdims=True)


def memory_kernel(
    reads,
    last_ref,
    q_ref,
    kt_ref,
    vt_ref,
    vb_ref,
    local_ref,
    wo_ref,
    x_ref,
    rows_ref,
    mix_ref,
    mk_ref,
    mv_ref,
    lse_ref,
    middle_ref,
    normed_ref,
    basis_t_ref,
    basis,
    turned,
    acc,
):
    step = pl.program_id(0)

    @pl.when(step == 0)
    def _():
        last_len = last_ref[0:1, 0:1]
        basis[...] = basis_rows(last_len, False).astype(bf16)
        basis_t_ref[...] = basis_rows(last_len, True).astype(bf16)
        acc[...] = jnp.zeros_like(acc)

    mem_k = dot(basis[...], kt_ref[...]).astype(bf16)
    mem_v = (dot(basis[...], vt_ref[...]) + vb_ref[0:1]).astype(bf16)
    mk_ref[...] = mem_k
    mv_ref[...] = mem_v
    v_t = mem_v.T
    query = lax.broadcasted_iota(jnp.int32, (1, HALF), 1)
    reading = query < reads[0, 0]
    q = q_ref[...]
    for head in range(2):
        rows = slice(head * HD, (head + 1) * HD)
        s = dot_nt(mem_k, head_lanes(q, head)) * SCORE_LOG2
        top = jnp.max(s, axis=0, keepdims=True)
        e = jnp.exp2(s - top)
        total = jnp.sum(e, axis=0, keepdims=True)
        out = dot(v_t[rows], e.astype(bf16))
        turned[rows, :] = jnp.where(reading, out / total, 0.0)
        lse_ref[0, head : head + 1, :] = jnp.where(reading, top + jnp.log2(total), -MASKED)
    mixed = jnp.concatenate(
        [local_ref[:HALF] + turned[...].T, local_ref[HALF:]], axis=0
    ).astype(bf16)
    mix_ref[...] = mixed
    acc[...] += dot(mixed, wo_ref[...])

    @pl.when(step == PAIRS - 1)
    def _():
        middle = x_ref[...].astype(f32) + (acc[...] + rows_ref[0:1])
        middle_ref[...] = middle
        normed_ref[...] = layer_norm(middle, rows_ref[1:2], rows_ref[2:3]).astype(bf16)


def memory_attention(reads, last_rows, qkv, tail_kv, value_bias, local, attn_out, inputs, rows):
    whole = lambda shape: pl.BlockSpec(shape, lambda i: (0,) * len(shape))
    return pl.pallas_call(
        memory_kernel,
        grid=(PAIRS,),
        in_specs=[
            pl.BlockSpec(memory_space=pltpu.SMEM),
            whole((16, D)),
            pl.BlockSpec((HALF, LANES), lambda i: (0, i)),
            pl.BlockSpec((HALF, LANES), lambda i: (0, i)),
            pl.BlockSpec((HALF, LANES), lambda i: (0, PAIRS + i)),
            pl.BlockSpec((8, LANES), lambda i: (0, i)),
            pl.BlockSpec((L, LANES), lambda i: (0, i)),
            pl.BlockSpec((LANES, D), lambda i: (i, 0)),
            whole((L, D)),
            whole((8, D)),
        ],
        out_specs=[
            pl.BlockSpec((L, LANES), lambda i: (0, i)),
            pl.BlockSpec((NB, LANES), lambda i: (0, i)),
            pl.BlockSpec((NB, LANES), lambda i: (0, i)),
            pl.BlockSpec((1, 8, HALF), lambda i: (i, 0, 0)),
            whole((L, D)),
            whole((L, D)),
            whole((HALF, NB)),
        ],
        out_shape=[
            jax.ShapeDtypeStruct((L, D), bf16),
            jax.ShapeDtypeStruct((NB, D), bf16),
            jax.ShapeDtypeStruct((NB, D), bf16),
            jax.ShapeDtypeStruct((PAIRS, 8, HALF), f32),
            jax.ShapeDtypeStruct((L, D), f32),
            jax.ShapeDtypeStruct((L, D), bf16),
            jax.ShapeDtypeStruct((HALF, NB), bf16),
        ],
        scratch_shapes=[
            pltpu.VMEM((NB, HALF), bf16),
            pltpu.VMEM((LANES, HALF), f32),
            pltpu.VMEM((L, D), f32),
        ],
        cost_estimate=pl.CostEstimate(
            flops=H * 16 * HALF * HALF * 256, bytes_accessed=16 * L * D, transcendentals=H * L * HALF
        ),
        name="memory_attention",
    )(reads, last_rows, qkv, tail_kv, tail_kv, value_bias, local, attn_out, inputs, rows)


def mlp_kernel(
    x_ref, ct_ref, wi_ref, bi_ref, wo_ref, hid_ref, dpre_ref, bias_ref, y_ref, dx_ref, y_acc, dx_acc
):
    step = pl.program_id(0)
    pre = dot(x_ref[...], wi_ref[...]) + bi_ref[0:1]
    squared = pre * pre
    tanh = jnp.tanh(pre * (0.7978845608028654 + 0.7978845608028654 * 0.044715 * squared))
    half = 0.5 * pre
    hidden = (half + half * tanh).astype(bf16)
    slope = (
        0.5
        + 0.5 * tanh
        + half
        * (1.0 - tanh * tanh)
        * (0.7978845608028654 + 3 * 0.7978845608028654 * 0.044715 * squared)
    )
    d_pre = (slope * dot_nt(ct_ref[...], wo_ref[...])).astype(bf16)
    hid_ref[...] = hidden
    dpre_ref[...] = d_pre
    bias_ref[...] = jnp.broadcast_to(
        jnp.sum(d_pre.astype(f32), axis=0, keepdims=True), bias_ref.shape
    )
    y = dot(hidden, wo_ref[...])
    dx = dot_nt(d_pre, wi_ref[...])

    @pl.when(step == 0)
    def _():
        y_acc[...] = y
        dx_acc[...] = dx

    @pl.when(step > 0)
    def _():
        y_acc[...] += y
        dx_acc[...] += dx

    @pl.when(step == pl.num_programs(0) - 1)
    def _():
        y_ref[...] = y_acc[...].astype(bf16)
        dx_ref[...] = dx_acc[...].astype(bf16)


def mlp_block(rows, cotangent, mlp_in, bias_rows, mlp_out):
    count, hidden = rows.shape[0], mlp_in.shape[1]
    tile = 256 if hidden % 256 == 0 else 128
    fixed = pl.BlockSpec((count, D), lambda i: (0, 0))
    across = pl.BlockSpec((count, tile), lambda i: (0, i))
    return pl.pallas_call(
        mlp_kernel,
        grid=(hidden // tile,),
        in_specs=[
            fixed,
            fixed,
            pl.BlockSpec((D, tile), lambda i: (0, i)),
            pl.BlockSpec((8, tile), lambda i: (0, i)),
            pl.BlockSpec((tile, D), lambda i: (i, 0)),
        ],
        out_specs=[across, across, pl.BlockSpec((8, tile), lambda i: (0, i)), fixed, fixed],
        out_shape=[
            jax.ShapeDtypeStruct((count, hidden), bf16),
            jax.ShapeDtypeStruct((count, hidden), bf16),
            jax.ShapeDtypeStruct((8, hidden), f32),
            jax.ShapeDtypeStruct((count, D), bf16),
            jax.ShapeDtypeStruct((count, D), bf16),
        ],
        scratch_shapes=[pltpu.VMEM((count, D), f32), pltpu.VMEM((count, D), f32)],
        cost_estimate=pl.CostEstimate(
            flops=8 * count * D * hidden,
            bytes_accessed=4 * D * hidden + 4 * count * hidden + 8 * count * D,
            transcendentals=count * hidden,
        ),
        name="mlp_block",
    )(rows, cotangent, mlp_in, bias_rows, mlp_out)


def backward_kernel(
    lens,
    q_ref,
    k_ref,
    v_ref,
    mk_ref,
    mv_ref,
    db_ref,
    wo_ref,
    ll_ref,
    lm_ref,
    bt_ref,
    dqkv_ref,
    dtail_ref,
    sums_ref,
    mask,
    turned,
    dk_acc,
    dv_acc,
):
    @pl.when(pl.program_id(0) == 0)
    def _():
        fill_mask(lens, mask)

    q, k, v = q_ref[...], k_ref[...], v_ref[...]
    mem_k, mem_v = mk_ref[...], mv_ref[...]
    d_mix = dot_nt(db_ref[...], wo_ref[...]).astype(bf16)
    k_t, mk_t = k.T, mem_k.T
    d_mem_k = d_mem_v = None

    def one(keys, values, q_part, d_part, lse, extra):
        s = dot_nt(keys, q_part) * SCORE_LOG2
        if extra is not None:
            s = s + extra
        weights = jnp.exp2(s - lse)
        d_weights = dot_nt(values, d_part)
        inner = jnp.sum(weights * d_weights, axis=0, keepdims=True)
        d_scores = (weights * (d_weights - inner)).astype(bf16)
        return d_scores, dot(d_scores, q_part), dot(weights.astype(bf16), d_part)

    for head in range(2):
        rows = slice(head * HD, (head + 1) * HD)
        q_head, d_head = head_lanes(q, head), head_lanes(d_mix, head)
        for part in range(2):
            keys = HALF * (part + 1)
            cols = slice(part * HALF, (part + 1) * HALF)
            ds, dk, dv = one(
                k[:keys],
                v[:keys],
                q_head[cols],
                d_head[cols],
                ll_ref[0, head : head + 1, cols],
                mask[:keys, cols],
            )
            dq = dot(k_t[rows, :keys], ds)
            if part == 0:
                ds, d_key, d_value = one(
                    mem_k, mem_v, q_head[cols], d_head[cols], lm_ref[0, head : head + 1, :], None
                )
                dq = dq + dot(mk_t[rows], ds)
                d_mem_k = d_key if d_mem_k is None else d_mem_k + d_key
                d_mem_v = d_value if d_mem_v is None else d_mem_v + d_value
            turned[rows, cols] = dq
            if head == 0 and part == 0:
                dk_acc[:HALF] = dk
                dv_acc[:HALF] = dv
            elif head == 0:
                dk_acc[:HALF] += dk[:HALF]
                dv_acc[:HALF] += dv[:HALF]
                dk_acc[HALF:] = dk[HALF:]
                dv_acc[HALF:] = dv[HALF:]
            else:
                dk_acc[:keys] += dk
                dv_acc[:keys] += dv
    scale = HD**-0.5
    d_q = (turned[...].T * scale).astype(bf16)
    d_v = dv_acc[...].astype(bf16)
    dqkv_ref[0] = d_q
    dqkv_ref[1] = (dk_acc[...] * scale).astype(bf16)
    dqkv_ref[2] = d_v
    d_mem_k = (d_mem_k * scale).astype(bf16)
    d_mem_v = d_mem_v.astype(bf16)
    dtail_ref[0] = dot(bt_ref[...], d_mem_k).astype(bf16)
    dtail_ref[1] = dot(bt_ref[...], d_mem_v).astype(bf16)
    sums_ref[0:1] = jnp.sum(d_q.astype(f32), axis=0, keepdims=True)
    sums_ref[1:2] = jnp.sum(d_v.astype(f32), axis=0, keepdims=True) + jnp.sum(
        d_mem_v.astype(f32), axis=0, keepdims=True
    )


def attention_backward(lens, qkv, mem_k, mem_v, d_branch, attn_out, lse_local, lse_mem, basis_t):
    column = lambda k: pl.BlockSpec((L, LANES), lambda i: (0, k * PAIRS + i))
    whole = lambda shape: pl.BlockSpec(shape, lambda i: (0,) * len(shape))
    return pl.pallas_call(
        backward_kernel,
        grid=(PAIRS,),
        in_specs=[
            pl.BlockSpec(memory_space=pltpu.SMEM),
            column(0),
            column(1),
            column(2),
            column(0),
            column(0),
            whole((L, D)),
            pl.BlockSpec((LANES, D), lambda i: (i, 0)),
            pl.BlockSpec((1, 8, L), lambda i: (i, 0, 0)),
            pl.BlockSpec((1, 8, HALF), lambda i: (i, 0, 0)),
            whole((HALF, NB)),
        ],
        out_specs=[
            pl.BlockSpec((3, L, LANES), lambda i: (0, 0, i)),
            pl.BlockSpec((2, HALF, LANES), lambda i: (0, 0, i)),
            pl.BlockSpec((8, LANES), lambda i: (0, i)),
        ],
        out_shape=[
            jax.ShapeDtypeStruct((3, L, D), bf16),
            jax.ShapeDtypeStruct((2, HALF, D), bf16),
            jax.ShapeDtypeStruct((8, D), f32),
        ],
        scratch_shapes=[
            pltpu.VMEM((L, L), f32),
            pltpu.VMEM((LANES, L), f32),
            pltpu.VMEM((L, LANES), f32),
            pltpu.VMEM((L, LANES), f32),
        ],
        cost_estimate=pl.CostEstimate(
            flops=H * 56 * HALF * HALF * 256, bytes_accessed=20 * L * D, transcendentals=H * L * L
        ),
        name="attention_backward",
    )(lens, qkv, qkv, qkv, mem_k, mem_v, d_branch, attn_out, lse_local, lse_mem, basis_t)


def rotated(value, axis, by):
    count = lax.axis_size(axis)
    return lax.ppermute(value, axis, [(i, (i + by) % count) for i in range(count)])


def swapped(value, axis, bit):
    count = lax.axis_size(axis)
    return lax.ppermute(value, axis, [(i, i ^ (1 << bit)) for i in range(count)])


def axis_bits(axis):
    return [(axis, bit) for bit in range(lax.axis_size(axis).bit_length() - 1)]


def side(axis, bit):
    return (lax.axis_index(axis) >> bit) & 1


def halve(value, axis, bit):
    count = value.shape[0] // 2
    mine = side(axis, bit)
    kept = lax.dynamic_slice_in_dim(value, mine * count, count, 0)
    given = lax.dynamic_slice_in_dim(value, (1 - mine) * count, count, 0)
    got = swapped(given, axis, bit)
    return (kept.astype(f32) + got.astype(f32)).astype(value.dtype)


def double(value, axis, bit):
    got = swapped(value, axis, bit)
    first = side(axis, bit) == 0
    return jnp.concatenate([jnp.where(first, value, got), jnp.where(first, got, value)], axis=0)


def sum_rows(value):
    batch, mlp = axis_bits("batch"), axis_bits("mlp")
    core, rest = batch[:1], batch[2:]
    orders = (batch[1:2] + mlp, mlp + batch[1:2])
    for step in core:
        value = halve(value, *step)
    parts = jnp.split(value, 2, axis=0)
    for steps in zip(*orders):
        parts = [halve(part, *step) for part, step in zip(parts, steps)]
    value = jnp.concatenate(parts, axis=0)
    for step in rest:
        value = halve(value, *step)
    for step in rest[::-1]:
        value = double(value, *step)
    parts = jnp.split(value, 2, axis=0)
    for steps in zip(*(order[::-1] for order in orders)):
        parts = [double(part, *step) for part, step in zip(parts, steps)]
    value = jnp.concatenate(parts, axis=0)
    for step in core:
        value = double(value, *step)
    return value


def sum_small(value):
    for step in axis_bits("batch") + axis_bits("mlp"):
        value = value + swapped(value, *step)
    return value


def shards(
    inputs,
    doc_lengths,
    ln1_gain,
    ln1_bias,
    attn_in,
    qv_bias,
    attn_out,
    attn_out_bias,
    ln2_gain,
    second_norm_bias,
    mlp_in,
    mlp_in_bias,
    mlp_out,
    mlp_out_bias,
    cotangent,
):
    n_mlp = lax.axis_size("mlp")
    place = lax.axis_index("mlp")
    gain_one = ln1_gain.astype(f32)
    bias_one = ln1_bias.astype(f32)
    gain_two = ln2_gain.astype(f32)
    bias_two = second_norm_bias.astype(f32)

    own_tail = jnp.concatenate(
        [
            inputs[HALF:],
            jnp.broadcast_to(doc_lengths[:, NDOC - 1 :].astype(bf16), (16, D)),
        ],
        axis=0,
    )
    tail = rotated(own_tail, "mlp", 1)
    cotangents = [cotangent] + [rotated(cotangent, "mlp", by) for by in range(1, n_mlp)]

    activations = inputs.astype(f32)
    normed = layer_norm(activations, gain_one, bias_one).astype(bf16)
    zeros = jnp.zeros((D,), f32)
    qkv_bias = jnp.concatenate([qv_bias[0].astype(f32), zeros, qv_bias[1].astype(f32)])
    qkv = (dot(normed, attn_in) + qkv_bias).astype(bf16)
    local, lse_local = local_attention(doc_lengths, qkv)

    tail_rows = tail[:HALF].astype(f32)
    normed_tail = layer_norm(tail_rows, gain_one, bias_one).astype(bf16)
    tail_kv = dot(normed_tail, attn_in[:, D:]).astype(bf16)
    reads = jnp.where(place == 0, 0, doc_lengths[:, :1])
    value_bias = jnp.broadcast_to(qv_bias[1].astype(f32), (8, D))
    rows = jnp.concatenate(
        [
            jnp.stack([attn_out_bias.astype(f32), gain_two, bias_two]),
            jnp.zeros((5, D), f32),
        ]
    )
    mixture, mem_k, mem_v, lse_mem, middle, normed_two, basis_t = memory_attention(
        reads, tail[HALF:], qkv, tail_kv, value_bias, local, attn_out, inputs, rows
    )

    bias_rows = jnp.broadcast_to(mlp_in_bias.astype(f32), (8, mlp_in.shape[1]))
    result = None
    d_normed_two = None
    d_mlp_in = d_mlp_out = d_mlp_in_bias = None
    arrived = [normed_two] + [rotated(normed_two, "mlp", by) for by in range(1, n_mlp)]
    partial_results = []
    for by in range(n_mlp):
        hidden, d_pre, d_bias, y, dx = mlp_block(
            arrived[by], cotangents[by], mlp_in, bias_rows, mlp_out
        )
        if by:
            dx = rotated(dx, "mlp", -by)
        grad_in = lax.dot_general(
            arrived[by], d_pre, (((0,), (0,)), ((), ())), preferred_element_type=f32
        )
        grad_out = lax.dot_general(
            hidden, cotangents[by], (((0,), (0,)), ((), ())), preferred_element_type=f32
        )
        partial_results.append(y)
        if by:
            d_normed_two = d_normed_two + dx.astype(f32)
            d_mlp_in, d_mlp_out = d_mlp_in + grad_in, d_mlp_out + grad_out
            d_mlp_in_bias = d_mlp_in_bias + d_bias[0]
        else:
            d_normed_two = dx.astype(f32)
            d_mlp_in, d_mlp_out, d_mlp_in_bias = grad_in, grad_out, d_bias[0]
    d_mlp_in, d_mlp_out = lax.psum((d_mlp_in.astype(bf16), d_mlp_out.astype(bf16)), "batch")

    upstream = cotangent.astype(f32)
    d_out_bias = jnp.sum(upstream, axis=0)
    d_middle_norm, d_ln2_gain, d_ln2_bias = norm_backward(middle, gain_two, bias_two, d_normed_two)
    d_middle = upstream + d_middle_norm
    d_branch = d_middle.astype(bf16)
    d_attn_out_bias = jnp.sum(d_branch, axis=0, dtype=f32)
    d_qkv, d_tail, sums = attention_backward(
        doc_lengths, qkv, mem_k, mem_v, d_branch, attn_out, lse_local, lse_mem, basis_t
    )
    over_rows = (((0,), (0,)), ((), ()))
    grads = [
        lax.dot_general(normed, d_qkv[0], over_rows, preferred_element_type=f32),
        lax.dot_general(normed, d_qkv[1], over_rows, preferred_element_type=f32)
        + lax.dot_general(normed_tail, d_tail[0], over_rows, preferred_element_type=f32),
        lax.dot_general(normed, d_qkv[2], over_rows, preferred_element_type=f32)
        + lax.dot_general(normed_tail, d_tail[1], over_rows, preferred_element_type=f32),
        lax.dot_general(mixture, d_branch, over_rows, preferred_element_type=f32),
    ]
    summed = sum_rows(jnp.concatenate([grad.astype(bf16) for grad in grads], axis=0))

    columns = [attn_in[:, i * D : (i + 1) * D] for i in range(3)]
    d_tail_rows = dot_nt(d_tail[0], columns[1]) + dot_nt(d_tail[1], columns[2])
    from_next = rotated(d_tail_rows.astype(bf16), "mlp", -1)
    d_normed = (
        dot_nt(d_qkv[0], columns[0]) + dot_nt(d_qkv[1], columns[1]) + dot_nt(d_qkv[2], columns[2])
    )
    d_normed = jnp.concatenate(
        [d_normed[:HALF], d_normed[HALF:] + from_next.astype(f32)], axis=0
    )
    d_in_norm, d_ln1_gain, d_ln1_bias = norm_backward(activations, gain_one, bias_one, d_normed)
    input_grad = (d_middle + d_in_norm).astype(bf16)

    result = partial_results[0].astype(f32)
    for by in range(1, n_mlp):
        result = result + rotated(partial_results[by], "mlp", -by).astype(f32)
    layer_output = (middle + (result + mlp_out_bias)).astype(bf16)

    hidden_count = mlp_in.shape[1]
    placed_bias = lax.dynamic_update_slice(
        jnp.zeros((n_mlp * hidden_count,), f32), d_mlp_in_bias, (place * hidden_count,)
    )
    vectors = jnp.concatenate(
        [
            jnp.stack(
                [d_ln1_gain, d_ln1_bias, d_attn_out_bias, d_ln2_gain, d_ln2_bias, d_out_bias]
            ),
            sums[:2],
            placed_bias.reshape(-1, D),
        ],
        axis=0,
    )
    vectors = sum_small(vectors)
    d_attn_in = jnp.concatenate([summed[i * D : (i + 1) * D] for i in range(3)], axis=1)
    return (
        layer_output,
        input_grad,
        vectors[0],
        vectors[1],
        d_attn_in.astype(f32),
        vectors[6:8],
        summed[3 * D :].astype(f32),
        vectors[2],
        vectors[3],
        vectors[4],
        d_mlp_in.astype(f32),
        lax.dynamic_slice(vectors[8:].reshape(-1), (place * hidden_count,), (hidden_count,)),
        d_mlp_out.astype(f32),
        vectors[5],
    )


def solution(mesh):
    rows, whole = P(("batch", "mlp"), None), P()
    columns, hidden, depth = P(None, "mlp"), P("mlp"), P("mlp", None)
    return jax.shard_map(
        shards,
        mesh=mesh,
        in_specs=(rows, rows) + (whole,) * 8 + (columns, hidden, depth, whole, rows),
        out_specs=(rows, rows) + (whole,) * 8 + (columns, hidden, depth, whole),
        check_vma=False,
    )
```

time: 556 us -> 375 us (0.67)
  matrix products: 141 us -> 33.6 us
  blocking collectives: 76 us -> 0 us
  Pallas kernels: 0 us -> 74.9 us
  waiting for transfers between devices: 215 us -> 154 us
  starting transfers between devices: 7.71 us -> 36.3 us
  other arithmetic: 59.9 us -> 40.6 us
  local copies, waits for them, and re-layouts: 31.8 us -> 16.2 us
    dot_general x29 -> x17, matrix products: 141 us -> 33.6 us  [the longest x2 8.98 us: dot(): return jnp.dot(a, b, preferred_element_type=f32)]
    psum x2 -> x0, blocking collectives: 76 us -> none  [the longest x1 41.2 us: shards(): lax.psum((d_attn_in, d_qv_bias, d_attn_out, d_attn_out_bias, d_ln1_gain,...]
    pallas_call x0 -> x5, Pallas kernels: none -> 74.9 us  [the longest x2 25.2 us: mlp_block(): pl.pallas_call(mlp_kernel, grid=(hidden // tile,), in_specs=[fixed, fixed...]
    ppermute x2 -> x25, waiting for transfers between devices: 33.7 us -> 107 us  [the longest x19 62.4 us: swapped(): return lax.ppermute(value, axis, [(i, i ^ 1 << bit) for i in range(count)])]
    psum x2 -> x1, waiting for transfers between devices: 104 us -> 47.5 us  [shards(): lax.psum((d_mlp_in.astype(bf16), d_mlp_out.astype(bf16)), 'batch')]
    all_gather x2 -> x0, waiting for transfers between devices: 48.1 us -> none  [the longest x1 26.8 us: shards(): gathered = lax.all_gather(normed_two, 'mlp', axis=0, tiled=True)]
    ppermute x2 -> x25, starting transfers between devices: 7.25 us -> 36.3 us  [the longest x19 27.6 us: swapped(): return lax.ppermute(value, axis, [(i, i ^ 1 << bit) for i in range(count)])]
    reduce_scatter x2 -> x0, waiting for transfers between devices: 28.3 us -> none  [the longest x1 26.5 us: shards(): lax.psum_scatter(jnp.dot(hidden_rows, mlp_out, preferred_element_type=jnp...]
  transfers between devices with their start and end apart: 8 -> 26, of which waited for: 7 -> 20; matrix products, arithmetic and copies ran while one was open for 29% -> 15% of each run, Pallas kernels for 0% -> 10%
where the time goes in v1:
time: 375 us; the launch traced here: 371 us
  waiting for transfers between devices  154 us (41%)
  Pallas kernels  74.9 us (20%)
  other arithmetic  40.6 us (11%)
  starting transfers between devices  36.3 us (10%)
  matrix products  33.6 us (9%)
  local copies, waits for them, and re-layouts  16.2 us (4%)
  between operations  15.1 us (4%)
    ppermute x19, waiting for transfers between devices, swapped(): return lax.ppermute(value, axis, [(i, i ^ 1 << bit) for i in range(count)])  62.4 us
    psum x1, waiting for transfers between devices, shards(): lax.psum((d_mlp_in.astype(bf16), d_mlp_out.astype(bf16)), 'batch')  47.5 us
    ppermute x6, waiting for transfers between devices, rotated(): lax.ppermute(value, axis, [(i, (i + by) % count) for i in range(count)])  44.4 us
    ppermute x19, starting transfers between devices, swapped(): return lax.ppermute(value, axis, [(i, i ^ 1 << bit) for i in range(count)])  27.6 us
    pallas_call x2, Pallas kernels, mlp_block(): pl.pallas_call(mlp_kernel, grid=(hidden // tile,), in_specs=[fixed, fixed...  25.2 us
    pallas_call x1, Pallas kernels, attention_backward(): pl.pallas_call(backward_kernel, grid=(PAIRS,), in_specs=[pl.BlockSpec(mem...  24.2 us
    pallas_call x1, Pallas kernels, memory_attention(): pl.pallas_call(memory_kernel, grid=(PAIRS,), in_specs=[pl.BlockSpec(memor...  13.8 us
    pallas_call x1, Pallas kernels, local_attention(): pl.pallas_call(local_kernel, grid=(PAIRS,), in_specs=[pl.BlockSpec(memory...  11.7 us
  transfers between devices with their start and end apart: 26, of which 20 were waited for; matrix products, arithmetic and copies ran while one was open for 15% of the time, Pallas kernels for 10%

profile of v1, /device:TPU:0, one launch (start us, length us, event | category | flops | bytes accessed | tf_op | source)
XLA Modules:
  0.0 371.0 jit_solution(9469564439454638489)
XLA Ops:
  10.4 3.1 collective-permute-start
  14.4 5.6 %fusion.q_ref.k_ref.v_ref = bf16[512,2304]{1,0:T(8,128)(2,1)} fusion(bf16[768,2304]{1,0:T(8,128)(2,1)} %param.19, f32[2304]{0:T(1024)S(1)} %pad_maximum_fusion.6, bf16[512,768]{1,0:T(8,128)(2,1)S(1)} %copy-done.1, f32[768]{0:T(1024)S(1)} %convert_element_type.177, f32[768]{0:T(1024)S(1)} %convert_element_type.176, f32[512]{0:T(512)S(1)} %fusion.54, ...), kind=kOutput, calls=%fused_computation.5 | convolution fusion | flops 1816657920 | bytes 6704128 | tf_op jit(solution)/shard_map/dot_general | solution.py:29
  20.7 11.7 %local_attention.1 = (f32[512,768]{1,0:T(8,128)}, f32[6,8,512]{2,1,0:T(8,128)}) custom-call(s32[1,3]{1,0:T(1,128)} %lens.3, bf16[512,2304]{1,0:T(8,128)(2,1)} %fusion.q_ref.k_ref.v_ref, bf16[512,2304]{1,0:T(8,128)(2,1)} %fusion.q_ref.k_ref.v_ref, bf16[512,2304]{1,0:T(8,128)(2,1)} %fusion.q_ref.k_ref.v_ref), custom_call_target="tpu_custom_call" | custom-call | flops 2415919104 | bytes 3145728 | tf_op jit(solution)/shard_map/local_attention/pallas_call | solution.py:87
  33.4 3.4 convolution_convert_fusion.kt_ref.vt_ref
  37.4 13.8 %memory_attention.1 = (bf16[512,768]{1,0:T(8,128)(2,1)}, bf16[512,768]{1,0:T(8,128)(2,1)}, bf16[512,768]{1,0:T(8,128)(2,1)}, f32[6,8,256]{2,1,0:T(8,128)}, f32[5...) custom-call(s32[1,1]{1,0:T(1,128)S(6)} %select_n.133.reads, bf16[16,768]{1,0:T(8,128)(2,1)} %slice.139.last_ref, ...), custom_call_target="tpu_custom_call" | custom-call | flops 3221225472 | bytes 6291456 | tf_op jit(solution)/shard_map/memory_attention/pallas_call | solution.py:178
  51.3 2.0 collective-permute-start.1
  54.9 15.7 %collective-permute-done.1.x_ref = bf16[512,768]{1,0:T(8,128)(2,1)S(1)} collective-permute-done((bf16[512,768]{1,0:T(8,128)(2,1)}, bf16[512,768]{1,0:T(8,128)(2,1)S(1)}, u32[]{:S(2)}, u32[]{:S(2)}) %collective-permute-start.1) | collective-permute-done | bytes 786464 | tf_op jit(solution)/shard_map/ppermute | solution.py:431
  71.5 12.6 %mlp_block.3 = (bf16[512,1536]{1,0:T(8,128)(2,1)}, bf16[512,1536]{1,0:T(8,128)(2,1)}, f32[8,1536]{1,0:T(8,128)}, bf16[512,768]{1,0:T(8,128)(2,1)}, bf16[512,768]{1,0:T(8,128)(2,1)}) custom-call(bf16[512,768]{1,0:T(8,128)(2,1)} %copy-done.25, bf16[512,768]{1,0:T(8,128)(2,1)} %copy-done.22, bf16[768,1536]{1,0:T(8,128)(2,1)} %wi_ref.3, ...), custom_call_target="tpu_custom_call" | custom-call | flops 4831838208 | bytes 11010048 | tf_op jit(solution)/shard_map/mlp_block/pallas_call | solution.py:269
  84.0 1.7 collective-permute-start.4
  85.8 12.6 %mlp_block.2 = (bf16[512,1536]{1,0:T(8,128)(2,1)}, bf16[512,1536]{1,0:T(8,128)(2,1)}, f32[8,1536]{1,0:T(8,128)}, bf16[512,768]{1,0:T(8,128)(2,1)}, bf16[512,768]{1,0:T(8,128)(2,1)}) custom-call(bf16[512,768]{1,0:T(8,128)(2,1)} %get-tuple-element.38.x_ref, bf16[512,768]{1,0:T(8,128)(2,1)} %ct_ref.1, bf16[768,1536]{1,0:T(8,128)(2,1)} %wi_ref.3, ...), custom_call_target="tpu_custom_call" | custom-call | flops 4831838208 | bytes 11010048 | tf_op jit(solution)/shard_map/mlp_block/pallas_call | solution.py:269
  99.4 5.3 %collective-permute-done.4 = bf16[512,768]{1,0:T(8,128)(2,1)S(1)} collective-permute-done((bf16[512,768]{1,0:T(8,128)(2,1)}, bf16[512,768]{1,0:T(8,128)(2,1)S(1)}, u32[]{:S(2)}, u32[]{:S(2)}) %collective-permute-start.4) | collective-permute-done | bytes 786464 | tf_op jit(solution)/shard_map/ppermute | solution.py:431
  105.5 13.8 %collective-permute-done.3 = bf16[512,768]{1,0:T(8,128)(2,1)S(1)} collective-permute-done((bf16[512,768]{1,0:T(8,128)(2,1)S(1)}, bf16[512,768]{1,0:T(8,128)(2,1)S(1)}, u32[]{:S(2)}, u32[]{:S(2)}) %collective-permute-start.3) | collective-permute-done | bytes 786464 | tf_op jit(solution)/shard_map/ppermute | solution.py:431
  119.3 1.8 fusion.66
  122.5 24.2 %attention_backward.1 = (bf16[3,512,768]{2,1,0:T(8,128)(2,1)}, bf16[2,256,768]{2,1,0:T(8,128)(2,1)}, f32[8,768]{1,0:T(8,128)}) custom-call(s32[1,3]{1,0:T(1,128)} %lens.3, bf16[512,2304]{1,0:T(8,128)(2,1)} %fusion.q_ref.k_ref.v_ref, bf16[512,2304]{1,0:T(8,128)(2,1)} %fusion.q_ref.k_ref.v_ref, bf16[512,2304]{1,0:T(8,128)(2,1)} %fusion.q_ref.k_ref.v_ref, ...), custom_call_target="tpu_custom_call" | custom-call | flops 11274289152 | bytes 7864320 | tf_op jit(solution)/shard_map/attention_backward/pallas_call | solution.py:390
  146.8 2.3 convolution_convert_fusion.2
  154.8 1.7 constant_dynamic-slice_fusion.5
  157.7 4.9 %collective-permute-done.11 = bf16[1536,768]{1,0:T(8,128)(2,1)} collective-permute-done((bf16[1536,768]{1,0:T(8,128)(2,1)}, bf16[1536,768]{1,0:T(8,128)(2,1)}, u32[]{:S(2)}, u32[]{:S(2)}) %collective-permute-start.11) | collective-permute-done | bytes 2359328 | tf_op jit(solution)/shard_map/ppermute | solution.py:436
  162.6 3.0 add_convert_fusion.2
  170.6 11.7 %collective-permute-done.12 = bf16[384,768]{1,0:T(8,128)(2,1)} collective-permute-done((bf16[384,768]{1,0:T(8,128)(2,1)S(1)}, bf16[384,768]{1,0:T(8,128)(2,1)}, u32[]{:S(2)}, u32[]{:S(2)}) %collective-permute-start.12) | collective-permute-done | bytes 589856 | tf_op jit(solution)/shard_map/ppermute | solution.py:436
  187.8 1.6 collective-permute-start.15
  189.4 3.5 collective-permute-done.13
  194.0 1.8 collective-permute-done.15
  197.1 1.6 collective-permute-start.16
  198.8 3.6 fusion.70
  202.4 1.8 collective-permute-done.16
  204.6 2.7 collective-permute-start.17
  208.7 3.8 %collective-permute-done.17 = bf16[96,768]{1,0:T(8,128)(2,1)S(1)} collective-permute-done((bf16[96,768]{1,0:T(8,128)(2,1)S(1)}, bf16[96,768]{1,0:T(8,128)(2,1)S(1)}, u32[]{:S(2)}, u32[]{:S(2)}) %collective-permute-start.17) | collective-permute-done | bytes 147488 | tf_op jit(solution)/shard_map/ppermute | solution.py:436
  213.7 2.9 add_convert_fusion.1
  220.5 5.2 %collective-permute-start.19 = (bf16[192,768]{1,0:T(8,128)(2,1)}, bf16[192,768]{1,0:T(8,128)(2,1)}, u32[]{:S(2)}, u32[]{:S(2)}) collective-permute-start(bf16[192,768]{1,0:T(8,128)(2,1)} %pad_maximum_fusion.5), channel_id=1, source_target_pairs={{0,8},{2,10},{4,12},{6,14},{8,0},{10,2},{12,4},{14,6},{16,24},{18,... | collective-permute-start | bytes 884744 | tf_op jit(solution)/shard_map/ppermute | solution.py:436
  225.8 5.2 %add_convert_fusion = bf16[1536,768]{1,0:T(8,128)(2,1)} fusion(f32[1536,768]{1,0:T(8,128)} %fusion.70, bf16[512,1536]{1,0:T(8,128)(2,1)S(1)} %copy-done.19, bf16[512,768]{1,0:T(8,128)(2,1)S(1)} %copy-done.23), kind=kOutput, calls=%fused_computation.2 | convolution fusion | flops 1210318848 | bytes 9437184 | tf_op jit(solution)/shard_map/dot_general | solution.py:562
  232.6 2.3 fusion.21
  236.5 5.5 %collective-permute-done.20 = bf16[192,768]{1,0:T(8,128)(2,1)S(1)} collective-permute-done((bf16[192,768]{1,0:T(8,128)(2,1)S(1)}, bf16[192,768]{1,0:T(8,128)(2,1)S(1)}, u32[]{:S(2)}, u32[]{:S(2)}) %collective-permute-start.20) | collective-permute-done | bytes 294944 | tf_op jit(solution)/shard_map/ppermute | solution.py:436
  243.7 6.5 %collective-permute-done.22 = bf16[192,768]{1,0:T(8,128)(2,1)S(1)} collective-permute-done((bf16[192,768]{1,0:T(8,128)(2,1)S(1)}, bf16[192,768]{1,0:T(8,128)(2,1)S(1)}, u32[]{:S(2)}, u32[]{:S(2)}) %collective-permute-start.22) | collective-permute-done | bytes 294944 | tf_op jit(solution)/shard_map/ppermute | solution.py:436
  252.9 8.9 %collective-permute-done.21 = bf16[384,768]{1,0:T(8,128)(2,1)S(1)} collective-permute-done((bf16[384,768]{1,0:T(8,128)(2,1)S(1)}, bf16[384,768]{1,0:T(8,128)(2,1)S(1)}, u32[]{:S(2)}, u32[]{:S(2)}) %collective-permute-start.21) | collective-permute-done | bytes 589856 | tf_op jit(solution)/shard_map/ppermute | solution.py:436
  262.3 1.7 pad_maximum_fusion.1
  267.4 9.6 %collective-permute-done.5 = bf16[256,768]{1,0:T(8,128)(2,1)S(1)} collective-permute-done((bf16[256,768]{1,0:T(8,128)(2,1)S(1)}, bf16[256,768]{1,0:T(8,128)(2,1)S(1)}, u32[]{:S(2)}, u32[]{:S(2)}) %collective-permute-start.5) | collective-permute-done | bytes 393248 | tf_op jit(solution)/shard_map/ppermute | solution.py:431
  279.0 1.7 convert_reduce_fusion
  283.6 2.6 collective-permute-done.7
  287.2 3.6 collective-permute-done.8
  290.7 2.4 collective-permute-start.9
  293.1 2.6 collective-permute-done.9
  297.0 2.9 collective-permute-done.10
  301.9 47.5 %all-reduce.4.cloned.1.call-done = (bf16[768,1536]{1,0:T(8,128)(2,1)}, bf16[1536,768]{1,0:T(8,128)(2,1)}) async-done(((bf16[768,1536]{1,0:T(8,128)(2,1)}, bf16[1536,768]{1,0:T(8,128)(2,1)}), (bf16[768,1536]{1,0:T(8,128)(2,1)}, bf16[1536,768]{1,0:T(8,128)(2,1)})) %all-reduce.4.cloned.1.call-update) | async-done | bytes 4718608 | tf_op jit(solution)/shard_map/psum | solution.py:573
  349.4 4.6 %convert_element_type.229 = f32[768,1536]{1,0:T(8,128)} convert(bf16[768,1536]{1,0:T(8,128)(2,1)} %get-tuple-element.71) | non-fusion elementwise | flops 1179648 | bytes 7077888 | tf_op jit(solution)/shard_map/convert_element_type | solution.py:639
  354.1 2.5 convert_element_type.231
  356.6 2.2 broadcast_select_fusion.1
  359.0 1.7 slice_convert_fusion
  360.7 3.2 maximum_convert_fusion
  (217 shorter events, 58.9 us)
Async XLA Ops:
  7.2 6.4 %copy-start.1 = (bf16[512,768]{1,0:T(8,128)(2,1)S(1)}, bf16[512,768]{1,0:T(8,128)(2,1)}, u32[]{:S(2)}) copy-start(bf16[512,768]{1,0:T(8,128)(2,1)} %x_ref.1) | copy-start | bytes 2359300
  7.2 6.3 %copy-start.6 = (bf16[512,768]{1,0:T(8,128)(2,1)S(1)}, bf16[512,768]{1,0:T(8,128)(2,1)}, u32[]{:S(2)}) copy-start(bf16[512,768]{1,0:T(8,128)(2,1)} %ct_ref.1) | copy-start | bytes 2359300
  7.2 342.2 %all-reduce.4.cloned.1.call-start = ((), (), s32[]{:S(2)}) async-start(), calls=%async_computation | async-start | bytes 9437184 | tf_op jit(solution)/shard_map/psum | solution.py:573
  8.6 5.6 %copy-start.38 = (bf16[768]{0:T(1024)(128)(2,1)S(1)}, bf16[768]{0:T(1024)(128)(2,1)}, u32[]{:S(2)}) copy-start(bf16[768]{0:T(1024)(128)(2,1)} %param.17) | copy-start | bytes 4612
  8.6 5.6 %copy-start.39 = (bf16[768]{0:T(1024)(128)(2,1)S(1)}, bf16[768]{0:T(1024)(128)(2,1)}, u32[]{:S(2)}) copy-start(bf16[768]{0:T(1024)(128)(2,1)} %param.18) | copy-start | bytes 4612
  8.6 5.6 %copy-start.35 = (bf16[2,768]{1,0:T(2,128)(2,1)S(1)}, bf16[2,768]{1,0:T(2,128)(2,1)}, u32[]{:S(2)}) copy-start(bf16[2,768]{1,0:T(2,128)(2,1)} %param.20) | copy-start | bytes 9220
  8.6 5.7 %copy-start.43 = (s32[1,3]{1,0:T(1,128)S(1)}, s32[1,3]{1,0:T(1,128)}, u32[]{:S(2)}) copy-start(s32[1,3]{1,0:T(1,128)} %lens.3) | copy-start | bytes 40
  10.4 21.9 %collective-permute-start = (bf16[272,768]{1,0:T(8,128)(2,1)S(1)}, bf16[272,768]{1,0:T(8,128)(2,1)S(1)}, u32[]{:S(2)}, u32[]{:S(2)}) collective-permute-start(bf16[272,768]{1,0:T(8,128)(2,1)S(1)} %concatenate.36), channel_id=1, source_target_pairs={{0,1},{1,0},{2,3},{3,2},{4,5},{5,4},{6,7},{7,6},{8,9},{9,8},{10,11... | collective-permute-start | bytes 1253384 | tf_op jit(solution)/shard_map/ppermute | solution.py:431
  13.5 41.4 %collective-permute-start.2 = (bf16[512,768]{1,0:T(8,128)(2,1)S(1)}, bf16[512,768]{1,0:T(8,128)(2,1)S(1)}, u32[]{:S(2)}, u32[]{:S(2)}) collective-permute-start(bf16[512,768]{1,0:T(8,128)(2,1)S(1)} %copy-done.6), channel_id=1, source_target_pairs={{0,1},{1,0},{2,3},{3,2},{4,5},{5,4},{6,7},{7,6},{8,9},{9,8},{10,11... | collective-permute-start | bytes 2359304 | tf_op jit(solution)/shard_map/ppermute | solution.py:431
  37.4 15.9 %copy-start.40 = (bf16[768]{0:T(1024)(128)(2,1)S(1)}, bf16[768]{0:T(1024)(128)(2,1)}, u32[]{:S(2)}) copy-start(bf16[768]{0:T(1024)(128)(2,1)} %param.28) | copy-start | bytes 4612
  51.3 19.3 %copy-start.37 = (bf16[1536]{0:T(1024)(128)(2,1)S(1)}, bf16[1536]{0:T(1024)(128)(2,1)}, u32[]{:S(2)}) copy-start(bf16[1536]{0:T(1024)(128)(2,1)} %param.26) | copy-start | bytes 9220
  51.3 19.3 %collective-permute-start.1 = (bf16[512,768]{1,0:T(8,128)(2,1)}, bf16[512,768]{1,0:T(8,128)(2,1)S(1)}, u32[]{:S(2)}, u32[]{:S(2)}) collective-permute-start(bf16[512,768]{1,0:T(8,128)(2,1)} %get-tuple-element.38.x_ref), channel_id=1, source_target_pairs={{0,1},{1,0},{2,3},{3,2},{4,5},{5,4},{6,7},{7,6},{8,9},{9,8},{10,11... | collective-permute-start | bytes 2359304 | tf_op jit(solution)/shard_map/ppermute | solution.py:431
  54.9 16.3 %copy-start.22 = (bf16[512,768]{1,0:T(8,128)(2,1)}, bf16[512,768]{1,0:T(8,128)(2,1)S(1)}, u32[]{:S(2)}) copy-start(bf16[512,768]{1,0:T(8,128)(2,1)S(1)} %collective-permute-done.2.ct_ref) | copy-start | bytes 2359300
  84.0 14.4 %copy-start.44 = (bf16[512,768]{1,0:T(8,128)(2,1)S(1)}, bf16[512,768]{1,0:T(8,128)(2,1)}, u32[]{:S(2)}) copy-start(bf16[512,768]{1,0:T(8,128)(2,1)} %get-tuple-element.40) | copy-start | bytes 2359300
  84.0 15.1 %copy-start = (f32[512,768]{1,0:T(8,128)S(1)}, f32[512,768]{1,0:T(8,128)}, u32[]{:S(2)}) copy-start(f32[512,768]{1,0:T(8,128)} %get-tuple-element.37) | copy-start | bytes 4718596
  84.0 20.7 %collective-permute-start.4 = (bf16[512,768]{1,0:T(8,128)(2,1)}, bf16[512,768]{1,0:T(8,128)(2,1)S(1)}, u32[]{:S(2)}, u32[]{:S(2)}) collective-permute-start(bf16[512,768]{1,0:T(8,128)(2,1)} %get-tuple-element.42), channel_id=1, source_target_pairs={{0,1},{1,0},{2,3},{3,2},{4,5},{5,4},{6,7},{7,6},{8,9},{9,8},{10,11... | collective-permute-start | bytes 2359304 | tf_op jit(solution)/shard_map/ppermute | solution.py:431
  98.4 6.3 %copy-start.15 = (bf16[512,768]{1,0:T(8,128)(2,1)S(1)}, bf16[512,768]{1,0:T(8,128)(2,1)}, u32[]{:S(2)}) copy-start(bf16[512,768]{1,0:T(8,128)(2,1)} %get-tuple-element.41) | copy-start | bytes 2359300
  98.4 20.9 %collective-permute-start.3 = (bf16[512,768]{1,0:T(8,128)(2,1)S(1)}, bf16[512,768]{1,0:T(8,128)(2,1)S(1)}, u32[]{:S(2)}, u32[]{:S(2)}) collective-permute-start(bf16[512,768]{1,0:T(8,128)(2,1)S(1)} %copy-done.44), channel_id=1, source_target_pairs={{0,1},{1,0},{2,3},{3,2},{4,5},{5,4},{6,7},{7,6},{8,9},{9,8},{10,11... | collective-permute-start | bytes 2359304 | tf_op jit(solution)/shard_map/ppermute | solution.py:431
  104.7 14.6 %copy-start.27 = (bf16[512,768]{1,0:T(8,128)(2,1)S(1)}, bf16[512,768]{1,0:T(8,128)(2,1)}, u32[]{:S(2)}) copy-start(bf16[512,768]{1,0:T(8,128)(2,1)} %get-tuple-element.39) | copy-start | bytes 2359300
  122.5 24.2 %copy-start.2 = (bf16[512,768]{1,0:T(8,128)(2,1)S(1)}, bf16[512,768]{1,0:T(8,128)(2,1)}, u32[]{:S(2)}) copy-start(bf16[512,768]{1,0:T(8,128)(2,1)} %x_ref.1) | copy-start | bytes 2359300
  157.7 4.9 %collective-permute-start.11 = (bf16[1536,768]{1,0:T(8,128)(2,1)}, bf16[1536,768]{1,0:T(8,128)(2,1)}, u32[]{:S(2)}, u32[]{:S(2)}) collective-permute-start(bf16[1536,768]{1,0:T(8,128)(2,1)} %constant_dynamic-slice_fusion.5), channel_id=1, source_target_pairs={{0,2},{2,0},{4,6},{6,4},{8,10},{10,8},{12,14},{14,12},{16,18},{18,... | collective-permute-start | bytes 7077896 | tf_op jit(solution)/shard_map/ppermute | solution.py:436
  166.8 15.5 %collective-permute-start.12 = (bf16[384,768]{1,0:T(8,128)(2,1)S(1)}, bf16[384,768]{1,0:T(8,128)(2,1)}, u32[]{:S(2)}, u32[]{:S(2)}) collective-permute-start(bf16[384,768]{1,0:T(8,128)(2,1)S(1)} %constant_dynamic-slice_fusion.4), channel_id=1, source_target_pairs={{0,4},{2,6},{4,0},{6,2},{8,12},{10,14},{12,8},{14,10},{16,20},{18,... | collective-permute-start | bytes 1769480 | tf_op jit(solution)/shard_map/ppermute | solution.py:436
  169.0 16.7 %collective-permute-start.14 = (bf16[384,768]{1,0:T(8,128)(2,1)}, bf16[384,768]{1,0:T(8,128)(2,1)}, u32[]{:S(2)}, u32[]{:S(2)}) collective-permute-start(bf16[384,768]{1,0:T(8,128)(2,1)} %constant_dynamic-slice_fusion.2), channel_id=1, source_target_pairs={{0,1},{1,0},{2,3},{3,2},{4,5},{5,4},{6,7},{7,6},{8,9},{9,8},{10,11... | collective-permute-start | bytes 1769480 | tf_op jit(solution)/shard_map/ppermute | solution.py:436
  184.4 8.5 %collective-permute-start.13 = (bf16[192,768]{1,0:T(8,128)(2,1)}, bf16[192,768]{1,0:T(8,128)(2,1)}, u32[]{:S(2)}, u32[]{:S(2)}) collective-permute-start(bf16[192,768]{1,0:T(8,128)(2,1)} %constant_dynamic-slice_fusion.3), channel_id=1, source_target_pairs={{0,1},{1,0},{2,3},{3,2},{4,5},{5,4},{6,7},{7,6},{8,9},{9,8},{10,11... | collective-permute-start | bytes 884744 | tf_op jit(solution)/shard_map/ppermute | solution.py:436
  187.8 8.0 %collective-permute-start.15 = (bf16[192,768]{1,0:T(8,128)(2,1)S(1)}, bf16[192,768]{1,0:T(8,128)(2,1)S(1)}, u32[]{:S(2)}, u32[]{:S(2)}) collective-permute-start(bf16[192,768]{1,0:T(8,128)(2,1)S(1)} %constant_dynamic-slice_fusion.1), channel_id=1, source_target_pairs={{0,4},{2,6},{4,0},{6,2},{8,12},{10,14},{12,8},{14,10},{16,20},{18,... | collective-permute-start | bytes 884744 | tf_op jit(solution)/shard_map/ppermute | solution.py:436
  189.4 9.4 %copy-start.18 = (bf16[512,1536]{1,0:T(8,128)(2,1)S(1)}, bf16[512,1536]{1,0:T(8,128)(2,1)}, u32[]{:S(2)}) copy-start(bf16[512,1536]{1,0:T(8,128)(2,1)} %get-tuple-element.56) | copy-start | bytes 4718596
  197.1 7.1 %collective-permute-start.16 = (bf16[192,768]{1,0:T(8,128)(2,1)S(1)}, bf16[192,768]{1,0:T(8,128)(2,1)S(1)}, u32[]{:S(2)}, u32[]{:S(2)}) collective-permute-start(bf16[192,768]{1,0:T(8,128)(2,1)S(1)} %fusion.52), channel_id=1, source_target_pairs={{0,8},{2,10},{4,12},{6,14},{8,0},{10,2},{12,4},{14,6},{16,24},{18,... | collective-permute-start | bytes 884744 | tf_op jit(solution)/shard_map/ppermute | solution.py:436
  198.8 8.5 %copy-start.21 = (bf16[512,1536]{1,0:T(8,128)(2,1)S(1)}, bf16[512,1536]{1,0:T(8,128)(2,1)}, u32[]{:S(2)}) copy-start(bf16[512,1536]{1,0:T(8,128)(2,1)} %get-tuple-element.55) | copy-start | bytes 4718596
  204.6 7.9 %collective-permute-start.17 = (bf16[96,768]{1,0:T(8,128)(2,1)S(1)}, bf16[96,768]{1,0:T(8,128)(2,1)S(1)}, u32[]{:S(2)}, u32[]{:S(2)}) collective-permute-start(bf16[96,768]{1,0:T(8,128)(2,1)S(1)} %constant_dynamic-slice_fusion), channel_id=1, source_target_pairs={{0,16},{2,18},{4,20},{6,22},{8,24},{10,26},{12,28},{14,30},{16,0},... | collective-permute-start | bytes 442376 | tf_op jit(solution)/shard_map/ppermute | solution.py:436
  207.3 6.4 %copy-start.20 = (bf16[512,1536]{1,0:T(8,128)(2,1)S(1)}, bf16[512,1536]{1,0:T(8,128)(2,1)}, u32[]{:S(2)}) copy-start(bf16[512,1536]{1,0:T(8,128)(2,1)} %get-tuple-element.54) | copy-start | bytes 4718596
  207.3 6.4 %copy-start.24 = (bf16[512,768]{1,0:T(8,128)(2,1)S(1)}, bf16[512,768]{1,0:T(8,128)(2,1)}, u32[]{:S(2)}) copy-start(bf16[512,768]{1,0:T(8,128)(2,1)} %get-tuple-element.38.x_ref) | copy-start | bytes 2359300
  212.6 6.2 %collective-permute-start.18 = (bf16[96,768]{1,0:T(8,128)(2,1)S(1)}, bf16[96,768]{1,0:T(8,128)(2,1)}, u32[]{:S(2)}, u32[]{:S(2)}) collective-permute-start(bf16[96,768]{1,0:T(8,128)(2,1)S(1)} %add_convert_fusion.12), channel_id=1, source_target_pairs={{0,16},{2,18},{4,20},{6,22},{8,24},{10,26},{12,28},{14,30},{16,0},... | collective-permute-start | bytes 442376 | tf_op jit(solution)/shard_map/ppermute | solution.py:436
  213.7 12.1 %copy-start.19 = (bf16[512,1536]{1,0:T(8,128)(2,1)S(1)}, bf16[512,1536]{1,0:T(8,128)(2,1)}, u32[]{:S(2)}) copy-start(bf16[512,1536]{1,0:T(8,128)(2,1)} %get-tuple-element.57) | copy-start | bytes 4718596
  218.0 7.7 %copy-start.23 = (bf16[512,768]{1,0:T(8,128)(2,1)S(1)}, bf16[512,768]{1,0:T(8,128)(2,1)}, u32[]{:S(2)}) copy-start(bf16[512,768]{1,0:T(8,128)(2,1)} %copy-done.22) | copy-start | bytes 2359300
  220.5 10.4 %collective-permute-start.19 = (bf16[192,768]{1,0:T(8,128)(2,1)}, bf16[192,768]{1,0:T(8,128)(2,1)}, u32[]{:S(2)}, u32[]{:S(2)}) collective-permute-start(bf16[192,768]{1,0:T(8,128)(2,1)} %pad_maximum_fusion.5), channel_id=1, source_target_pairs={{0,8},{2,10},{4,12},{6,14},{8,0},{10,2},{12,4},{14,6},{16,24},{18,... | collective-permute-start | bytes 884744 | tf_op jit(solution)/shard_map/ppermute | solution.py:436
  232.1 9.9 %collective-permute-start.20 = (bf16[192,768]{1,0:T(8,128)(2,1)S(1)}, bf16[192,768]{1,0:T(8,128)(2,1)S(1)}, u32[]{:S(2)}, u32[]{:S(2)}) collective-permute-start(bf16[192,768]{1,0:T(8,128)(2,1)S(1)} %get-tuple-element.98), channel_id=1, source_target_pairs={{0,1},{1,0},{2,3},{3,2},{4,5},{5,4},{6,7},{7,6},{8,9},{9,8},{10,11... | collective-permute-start | bytes 884744 | tf_op jit(solution)/shard_map/ppermute | solution.py:436
  234.9 15.2 %collective-permute-start.22 = (bf16[192,768]{1,0:T(8,128)(2,1)S(1)}, bf16[192,768]{1,0:T(8,128)(2,1)S(1)}, u32[]{:S(2)}, u32[]{:S(2)}) collective-permute-start(bf16[192,768]{1,0:T(8,128)(2,1)S(1)} %get-tuple-element.99), channel_id=1, source_target_pairs={{0,4},{2,6},{4,0},{6,2},{8,12},{10,14},{12,8},{14,10},{16,20},{18,... | collective-permute-start | bytes 884744 | tf_op jit(solution)/shard_map/ppermute | solution.py:436
  242.0 9.5 %copy-start.32 = (bf16[768,2304]{1,0:T(8,128)(2,1)S(1)}, bf16[768,2304]{1,0:T(8,128)(2,1)}, u32[]{:S(2)}) copy-start(bf16[768,2304]{1,0:T(8,128)(2,1)} %param.19) | copy-start | bytes 10616836
  242.1 9.5 %copy-start.30 = (bf16[2,256,768]{2,1,0:T(8,128)(2,1)S(1)}, bf16[2,256,768]{2,1,0:T(8,128)(2,1)}, u32[]{:S(2)}) copy-start(bf16[2,256,768]{2,1,0:T(8,128)(2,1)} %get-tuple-element.49) | copy-start | bytes 2359300
  242.1 19.7 %collective-permute-start.21 = (bf16[384,768]{1,0:T(8,128)(2,1)S(1)}, bf16[384,768]{1,0:T(8,128)(2,1)S(1)}, u32[]{:S(2)}, u32[]{:S(2)}) collective-permute-start(bf16[384,768]{1,0:T(8,128)(2,1)S(1)} %pad_maximum_fusion.3), channel_id=1, source_target_pairs={{0,4},{2,6},{4,0},{6,2},{8,12},{10,14},{12,8},{14,10},{16,20},{18,... | collective-permute-start | bytes 1769480 | tf_op jit(solution)/shard_map/ppermute | solution.py:436
  250.3 11.8 %collective-permute-start.23 = (bf16[384,768]{1,0:T(8,128)(2,1)S(1)}, bf16[384,768]{1,0:T(8,128)(2,1)S(1)}, u32[]{:S(2)}, u32[]{:S(2)}) collective-permute-start(bf16[384,768]{1,0:T(8,128)(2,1)S(1)} %pad_maximum_fusion.4), channel_id=1, source_target_pairs={{0,1},{1,0},{2,3},{3,2},{4,5},{5,4},{6,7},{7,6},{8,9},{9,8},{10,11... | collective-permute-start | bytes 1769480 | tf_op jit(solution)/shard_map/ppermute | solution.py:436
  264.1 92.5 %collective-permute-start.24 = (bf16[1536,768]{1,0:T(8,128)(2,1)}, bf16[1536,768]{1,0:T(8,128)(2,1)}, u32[]{:S(2)}, u32[]{:S(2)}) collective-permute-start(bf16[1536,768]{1,0:T(8,128)(2,1)} %pad_maximum_fusion.1), channel_id=1, source_target_pairs={{0,2},{2,0},{4,6},{6,4},{8,10},{10,8},{12,14},{14,12},{16,18},{18,... | collective-permute-start | bytes 7077896 | tf_op jit(solution)/shard_map/ppermute | solution.py:436
  265.4 11.5 %collective-permute-start.5 = (bf16[256,768]{1,0:T(8,128)(2,1)S(1)}, bf16[256,768]{1,0:T(8,128)(2,1)S(1)}, u32[]{:S(2)}, u32[]{:S(2)}) collective-permute-start(bf16[256,768]{1,0:T(8,128)(2,1)S(1)} %fusion.14), channel_id=1, source_target_pairs={{0,1},{1,0},{2,3},{3,2},{4,5},{5,4},{6,7},{7,6},{8,9},{9,8},{10,11... | collective-permute-start | bytes 1179656 | tf_op jit(solution)/shard_map/ppermute | solution.py:431
  280.7 1.3 collective-permute-start.6
  282.0 4.2 %collective-permute-start.7 = (f32[12,768]{1,0:T(8,128)S(1)}, f32[12,768]{1,0:T(8,128)S(1)}, u32[]{:S(2)}, u32[]{:S(2)}) collective-permute-start(f32[12,768]{1,0:T(8,128)S(1)} %add.221), channel_id=1, source_target_pairs={{0,4},{2,6},{4,0},{6,2},{8,12},{10,14},{12,8},{14,10},{16,20},{18,... | collective-permute-start | bytes 110600 | tf_op jit(solution)/shard_map/ppermute | solution.py:436
  286.2 4.5 %collective-permute-start.8 = (f32[12,768]{1,0:T(8,128)S(1)}, f32[12,768]{1,0:T(8,128)S(1)}, u32[]{:S(2)}, u32[]{:S(2)}) collective-permute-start(f32[12,768]{1,0:T(8,128)S(1)} %add.222), channel_id=1, source_target_pairs={{0,8},{2,10},{4,12},{6,14},{8,0},{10,2},{12,4},{14,6},{16,24},{18,... | collective-permute-start | bytes 110600 | tf_op jit(solution)/shard_map/ppermute | solution.py:436
  290.7 5.0 %collective-permute-start.9 = (f32[12,768]{1,0:T(8,128)S(1)}, f32[12,768]{1,0:T(8,128)S(1)}, u32[]{:S(2)}, u32[]{:S(2)}) collective-permute-start(f32[12,768]{1,0:T(8,128)S(1)} %add.223), channel_id=1, source_target_pairs={{0,16},{2,18},{4,20},{6,22},{8,24},{10,26},{12,28},{14,30},{16,0},... | collective-permute-start | bytes 110600 | tf_op jit(solution)/shard_map/ppermute | solution.py:436
  295.8 4.2 %collective-permute-start.10 = (f32[12,768]{1,0:T(8,128)S(1)}, f32[12,768]{1,0:T(8,128)S(1)}, u32[]{:S(2)}, u32[]{:S(2)}) collective-permute-start(f32[12,768]{1,0:T(8,128)S(1)} %add.224), channel_id=1, source_target_pairs={{0,1},{1,0},{2,3},{3,2},{4,5},{5,4},{6,7},{7,6},{8,9},{9,8},{10,11... | collective-permute-start | bytes 110600 | tf_op jit(solution)/shard_map/ppermute | solution.py:436
  (24 other events, 62.4 us)
Sparse Core Ops, SparseCore 0:
  231.1 118.2 all-reduce.3

commit v2 on v1

--- a/solution.py
+++ b/solution.py
@@ -59,10 +59,29 @@
     mask[...] = jnp.where((key <= query) & (key >= start), 0.0, MASKED)
 
 
-def local_kernel(lens, q_ref, k_ref, v_ref, out_ref, lse_ref, mask, turned):
-    @pl.when(pl.program_id(0) == 0)
+def local_kernel(
+    lens,
+    q_ref,
+    k_ref,
+    v_ref,
+    wo_ref,
+    x_ref,
+    rows_ref,
+    out_ref,
+    lse_ref,
+    mix_ref,
+    middle_ref,
+    normed_ref,
+    mask,
+    turned,
+    acc,
+):
+    step = pl.program_id(0)
+
+    @pl.when(step == 0)
     def _():
         fill_mask(lens, mask)
+        acc[...] = jnp.zeros_like(acc)
 
     q, k = q_ref[...], k_ref[...]
     v_t = v_ref[...].T
@@ -79,26 +98,61 @@
             out = dot(v_t[rows, :keys], e.astype(bf16))
             turned[rows, cols] = out / total
             lse_ref[0, head : head + 1, cols] = top + jnp.log2(total)
-    out_ref[...] = turned[...].T
-
-
-def local_attention(lens, qkv):
+    out_ref[...] = turned[:, :HALF].T
+    mixed = turned[:, HALF:].T.astype(bf16)
+    mix_ref[...] = mixed
+    acc[...] += dot(mixed, wo_ref[...])
+
+    @pl.when(step == PAIRS - 1)
+    def _():
+        finish_middle(x_ref, acc, rows_ref, middle_ref, normed_ref)
+
+
+def finish_middle(x_ref, acc, rows_ref, middle_ref, normed_ref):
+    middle = x_ref[...].astype(f32) + (acc[...] + rows_ref[0:1])
+    middle_ref[...] = middle
+    normed_ref[...] = layer_norm(middle, rows_ref[1:2], rows_ref[2:3]).astype(bf16)
+
+
+def local_attention(lens, qkv, attn_out, inputs, rows):
     column = lambda k: pl.BlockSpec((L, LANES), lambda i: (0, k * PAIRS + i))
+    upper = pl.BlockSpec((HALF, D), lambda i: (1, 0))
     return pl.pallas_call(
         local_kernel,
         grid=(PAIRS,),
-        in_specs=[pl.BlockSpec(memory_space=pltpu.SMEM), column(0), column(1), column(2)],
-        out_specs=[column(0), pl.BlockSpec((1, 8, L), lambda i: (i, 0, 0))],
+        in_specs=[
+            pl.BlockSpec(memory_space=pltpu.SMEM),
+            column(0),
+            column(1),
+            column(2),
+            pl.BlockSpec((LANES, D), lambda i: (i, 0)),
+            upper,
+            pl.BlockSpec((8, D), lambda i: (0, 0)),
+        ],
+        out_specs=[
+            pl.BlockSpec((HALF, LANES), lambda i: (0, i)),
+            pl.BlockSpec((1, 8, L), lambda i: (i, 0, 0)),
+            pl.BlockSpec((HALF, LANES), lambda i: (1, i)),
+            upper,
+            upper,
+        ],
         out_shape=[
+            jax.ShapeDtypeStruct((HALF, D), f32),
+            jax.ShapeDtypeStruct((PAIRS, 8, L), f32),
+            jax.ShapeDtypeStruct((L, D), bf16),
             jax.ShapeDtypeStruct((L, D), f32),
-            jax.ShapeDtypeStruct((PAIRS, 8, L), f32),
-        ],
-        scratch_shapes=[pltpu.VMEM((L, L), f32), pltpu.VMEM((LANES, L), f32)],
+            jax.ShapeDtypeStruct((L, D), bf16),
+        ],
+        scratch_shapes=[
+            pltpu.VMEM((L, L), f32),
+            pltpu.VMEM((LANES, L), f32),
+            pltpu.VMEM((HALF, D), f32),
+        ],
         cost_estimate=pl.CostEstimate(
             flops=H * 12 * HALF * HALF * 256, bytes_accessed=8 * L * D, transcendentals=H * L * L
         ),
         name="local_attention",
-    )(lens, qkv, qkv, qkv)
+    )(lens, qkv, qkv, qkv, attn_out, inputs, rows)
 
 
 def basis_rows(last_len, transposed):
@@ -123,6 +177,9 @@
     wo_ref,
     x_ref,
     rows_ref,
+    mix_whole,
+    middle_whole,
+    normed_whole,
     mix_ref,
     mk_ref,
     mv_ref,
@@ -160,21 +217,20 @@
         out = dot(v_t[rows], e.astype(bf16))
         turned[rows, :] = jnp.where(reading, out / total, 0.0)
         lse_ref[0, head : head + 1, :] = jnp.where(reading, top + jnp.log2(total), -MASKED)
-    mixed = jnp.concatenate(
-        [local_ref[:HALF] + turned[...].T, local_ref[HALF:]], axis=0
-    ).astype(bf16)
+    mixed = (local_ref[...] + turned[...].T).astype(bf16)
     mix_ref[...] = mixed
     acc[...] += dot(mixed, wo_ref[...])
 
     @pl.when(step == PAIRS - 1)
     def _():
-        middle = x_ref[...].astype(f32) + (acc[...] + rows_ref[0:1])
-        middle_ref[...] = middle
-        normed_ref[...] = layer_norm(middle, rows_ref[1:2], rows_ref[2:3]).astype(bf16)
-
-
-def memory_attention(reads, last_rows, qkv, tail_kv, value_bias, local, attn_out, inputs, rows):
+        finish_middle(x_ref, acc, rows_ref, middle_ref, normed_ref)
+
+
+def memory_attention(
+    reads, last_rows, qkv, tail_kv, value_bias, local, attn_out, inputs, rows, mixture, middle, normed
+):
     whole = lambda shape: pl.BlockSpec(shape, lambda i: (0,) * len(shape))
+    untouched = pl.BlockSpec(memory_space=pl.ANY)
     return pl.pallas_call(
         memory_kernel,
         grid=(PAIRS,),
@@ -185,18 +241,21 @@
             pl.BlockSpec((HALF, LANES), lambda i: (0, i)),
             pl.BlockSpec((HALF, LANES), lambda i: (0, PAIRS + i)),
             pl.BlockSpec((8, LANES), lambda i: (0, i)),
-            pl.BlockSpec((L, LANES), lambda i: (0, i)),
+            pl.BlockSpec((HALF, LANES), lambda i: (0, i)),
             pl.BlockSpec((LANES, D), lambda i: (i, 0)),
-            whole((L, D)),
+            whole((HALF, D)),
             whole((8, D)),
+            untouched,
+            untouched,
+            untouched,
         ],
         out_specs=[
-            pl.BlockSpec((L, LANES), lambda i: (0, i)),
+            pl.BlockSpec((HALF, LANES), lambda i: (0, i)),
             pl.BlockSpec((NB, LANES), lambda i: (0, i)),
             pl.BlockSpec((NB, LANES), lambda i: (0, i)),
             pl.BlockSpec((1, 8, HALF), lambda i: (i, 0, 0)),
-            whole((L, D)),
-            whole((L, D)),
+            whole((HALF, D)),
+            whole((HALF, D)),
             whole((HALF, NB)),
         ],
         out_shape=[
@@ -211,18 +270,32 @@
         scratch_shapes=[
             pltpu.VMEM((NB, HALF), bf16),
             pltpu.VMEM((LANES, HALF), f32),
-            pltpu.VMEM((L, D), f32),
-        ],
+            pltpu.VMEM((HALF, D), f32),
+        ],
+        input_output_aliases={10: 0, 11: 4, 12: 5},
         cost_estimate=pl.CostEstimate(
             flops=H * 16 * HALF * HALF * 256, bytes_accessed=16 * L * D, transcendentals=H * L * HALF
         ),
         name="memory_attention",
-    )(reads, last_rows, qkv, tail_kv, tail_kv, value_bias, local, attn_out, inputs, rows)
-
-
-def mlp_kernel(
-    x_ref, ct_ref, wi_ref, bi_ref, wo_ref, hid_ref, dpre_ref, bias_ref, y_ref, dx_ref, y_acc, dx_acc
-):
+    )(
+        reads,
+        last_rows,
+        qkv,
+        tail_kv,
+        tail_kv,
+        value_bias,
+        local,
+        attn_out,
+        inputs,
+        rows,
+        mixture,
+        middle,
+        normed,
+    )
+
+
+def mlp_kernel(x_ref, ct_ref, wi_ref, bi_ref, wo_ref, *refs):
+    hid_ref, dpre_ref, bias_ref, y_ref, dx_ref, y_acc, dx_acc = refs[-7:]
     step = pl.program_id(0)
     pre = dot(x_ref[...], wi_ref[...]) + bi_ref[0:1]
     squared = pre * pre
@@ -261,37 +334,39 @@
         dx_ref[...] = dx_acc[...].astype(bf16)
 
 
-def mlp_block(rows, cotangent, mlp_in, bias_rows, mlp_out):
+def mlp_block(rows, cotangent, part, mlp_in, bias_rows, mlp_out, total, place, kept):
     count, hidden = rows.shape[0], mlp_in.shape[1]
     tile = 256 if hidden % 256 == 0 else 128
     fixed = pl.BlockSpec((count, D), lambda i: (0, 0))
-    across = pl.BlockSpec((count, tile), lambda i: (0, i))
+    across = pl.BlockSpec((count, tile), lambda i: (place, i))
     return pl.pallas_call(
         mlp_kernel,
         grid=(hidden // tile,),
         in_specs=[
             fixed,
-            fixed,
+            pl.BlockSpec((count, D), lambda i: (part, 0)),
             pl.BlockSpec((D, tile), lambda i: (0, i)),
             pl.BlockSpec((8, tile), lambda i: (0, i)),
             pl.BlockSpec((tile, D), lambda i: (i, 0)),
-        ],
+        ]
+        + [pl.BlockSpec(memory_space=pl.ANY)] * len(kept),
         out_specs=[across, across, pl.BlockSpec((8, tile), lambda i: (0, i)), fixed, fixed],
         out_shape=[
-            jax.ShapeDtypeStruct((count, hidden), bf16),
-            jax.ShapeDtypeStruct((count, hidden), bf16),
+            jax.ShapeDtypeStruct((total, hidden), bf16),
+            jax.ShapeDtypeStruct((total, hidden), bf16),
             jax.ShapeDtypeStruct((8, hidden), f32),
             jax.ShapeDtypeStruct((count, D), bf16),
             jax.ShapeDtypeStruct((count, D), bf16),
         ],
         scratch_shapes=[pltpu.VMEM((count, D), f32), pltpu.VMEM((count, D), f32)],
+        input_output_aliases={5 + i: i for i in range(len(kept))},
         cost_estimate=pl.CostEstimate(
             flops=8 * count * D * hidden,
             bytes_accessed=4 * D * hidden + 4 * count * hidden + 8 * count * D,
             transcendentals=count * hidden,
         ),
         name="mlp_block",
-    )(rows, cotangent, mlp_in, bias_rows, mlp_out)
+    )(rows, cotangent, mlp_in, bias_rows, mlp_out, *kept)
 
 
 def backward_kernel(
@@ -384,12 +459,15 @@
     )
 
 
-def attention_backward(lens, qkv, mem_k, mem_v, d_branch, attn_out, lse_local, lse_mem, basis_t):
-    column = lambda k: pl.BlockSpec((L, LANES), lambda i: (0, k * PAIRS + i))
+def attention_backward(
+    first, pairs, lens, qkv, mem_k, mem_v, d_branch, attn_out, lse_local, lse_mem, basis_t
+):
+    column = lambda k: pl.BlockSpec((L, LANES), lambda i: (0, k * PAIRS + first + i))
     whole = lambda shape: pl.BlockSpec(shape, lambda i: (0,) * len(shape))
+    width = pairs * LANES
     return pl.pallas_call(
         backward_kernel,
-        grid=(PAIRS,),
+        grid=(pairs,),
         in_specs=[
             pl.BlockSpec(memory_space=pltpu.SMEM),
             column(0),
@@ -398,9 +476,9 @@
             column(0),
             column(0),
             whole((L, D)),
-            pl.BlockSpec((LANES, D), lambda i: (i, 0)),
-            pl.BlockSpec((1, 8, L), lambda i: (i, 0, 0)),
-            pl.BlockSpec((1, 8, HALF), lambda i: (i, 0, 0)),
+            pl.BlockSpec((LANES, D), lambda i: (first + i, 0)),
+            pl.BlockSpec((1, 8, L), lambda i: (first + i, 0, 0)),
+            pl.BlockSpec((1, 8, HALF), lambda i: (first + i, 0, 0)),
             whole((HALF, NB)),
         ],
         out_specs=[
@@ -409,9 +487,9 @@
             pl.BlockSpec((8, LANES), lambda i: (0, i)),
         ],
         out_shape=[
-            jax.ShapeDtypeStruct((3, L, D), bf16),
-            jax.ShapeDtypeStruct((2, HALF, D), bf16),
-            jax.ShapeDtypeStruct((8, D), f32),
+            jax.ShapeDtypeStruct((3, L, width), bf16),
+            jax.ShapeDtypeStruct((2, HALF, width), bf16),
+            jax.ShapeDtypeStruct((8, width), f32),
         ],
         scratch_shapes=[
             pltpu.VMEM((L, L), f32),
@@ -420,7 +498,9 @@
             pltpu.VMEM((L, LANES), f32),
         ],
         cost_estimate=pl.CostEstimate(
-            flops=H * 56 * HALF * HALF * 256, bytes_accessed=20 * L * D, transcendentals=H * L * L
+            flops=2 * pairs * 56 * HALF * HALF * 256,
+            bytes_accessed=20 * L * width,
+            transcendentals=2 * pairs * L * L,
         ),
         name="attention_backward",
     )(lens, qkv, qkv, qkv, mem_k, mem_v, d_branch, attn_out, lse_local, lse_mem, basis_t)
@@ -459,25 +539,14 @@
     return jnp.concatenate([jnp.where(first, value, got), jnp.where(first, got, value)], axis=0)
 
 
-def sum_rows(value):
-    batch, mlp = axis_bits("batch"), axis_bits("mlp")
-    core, rest = batch[:1], batch[2:]
-    orders = (batch[1:2] + mlp, mlp + batch[1:2])
-    for step in core:
+def scatter_sum(value, steps):
+    for step in steps:
         value = halve(value, *step)
-    parts = jnp.split(value, 2, axis=0)
-    for steps in zip(*orders):
-        parts = [halve(part, *step) for part, step in zip(parts, steps)]
-    value = jnp.concatenate(parts, axis=0)
-    for step in rest:
-        value = halve(value, *step)
-    for step in rest[::-1]:
-        value = double(value, *step)
-    parts = jnp.split(value, 2, axis=0)
-    for steps in zip(*(order[::-1] for order in orders)):
-        parts = [double(part, *step) for part, step in zip(parts, steps)]
-    value = jnp.concatenate(parts, axis=0)
-    for step in core:
+    return value
+
+
+def gather(value, steps):
+    for step in reversed(steps):
         value = double(value, *step)
     return value
 
@@ -527,87 +596,124 @@
     zeros = jnp.zeros((D,), f32)
     qkv_bias = jnp.concatenate([qv_bias[0].astype(f32), zeros, qv_bias[1].astype(f32)])
     qkv = (dot(normed, attn_in) + qkv_bias).astype(bf16)
-    local, lse_local = local_attention(doc_lengths, qkv)
+    rows = jnp.concatenate(
+        [
+            jnp.stack([attn_out_bias.astype(f32), gain_two, bias_two]),
+            jnp.zeros((5, D), f32),
+        ]
+    )
+    local, lse_local, mixture, middle, normed_two = local_attention(
+        doc_lengths, qkv, attn_out, inputs, rows
+    )
+    steps = range(1, n_mlp)
+    arrived_hi = [rotated(normed_two[HALF:], "mlp", by) for by in steps]
 
     tail_rows = tail[:HALF].astype(f32)
     normed_tail = layer_norm(tail_rows, gain_one, bias_one).astype(bf16)
     tail_kv = dot(normed_tail, attn_in[:, D:]).astype(bf16)
     reads = jnp.where(place == 0, 0, doc_lengths[:, :1])
     value_bias = jnp.broadcast_to(qv_bias[1].astype(f32), (8, D))
-    rows = jnp.concatenate(
-        [
-            jnp.stack([attn_out_bias.astype(f32), gain_two, bias_two]),
-            jnp.zeros((5, D), f32),
-        ]
-    )
     mixture, mem_k, mem_v, lse_mem, middle, normed_two, basis_t = memory_attention(
-        reads, tail[HALF:], qkv, tail_kv, value_bias, local, attn_out, inputs, rows
-    )
+        reads,
+        tail[HALF:],
+        qkv,
+        tail_kv,
+        value_bias,
+        local,
+        attn_out,
+        inputs,
+        rows,
+        mixture,
+        middle,
+        normed_two,
+    )
+    arrived_lo = [rotated(normed_two[:HALF], "mlp", by) for by in steps]
 
     bias_rows = jnp.broadcast_to(mlp_in_bias.astype(f32), (8, mlp_in.shape[1]))
-    result = None
-    d_normed_two = None
-    d_mlp_in = d_mlp_out = d_mlp_in_bias = None
-    arrived = [normed_two] + [rotated(normed_two, "mlp", by) for by in range(1, n_mlp)]
-    partial_results = []
-    for by in range(n_mlp):
+    kept = ()
+    d_mlp_in_bias = 0.0
+    returned_y, returned_dx = [], []
+    calls = [(by, part) for by in steps for part in (1, 0)]
+    for by, part in calls:
+        block = (arrived_lo, arrived_hi)[part][by - 1]
         hidden, d_pre, d_bias, y, dx = mlp_block(
-            arrived[by], cotangents[by], mlp_in, bias_rows, mlp_out
+            block, cotangents[by], part, mlp_in, bias_rows, mlp_out, n_mlp * L, 2 * by + part, kept
         )
-        if by:
-            dx = rotated(dx, "mlp", -by)
-        grad_in = lax.dot_general(
-            arrived[by], d_pre, (((0,), (0,)), ((), ())), preferred_element_type=f32
-        )
-        grad_out = lax.dot_general(
-            hidden, cotangents[by], (((0,), (0,)), ((), ())), preferred_element_type=f32
-        )
-        partial_results.append(y)
-        if by:
-            d_normed_two = d_normed_two + dx.astype(f32)
-            d_mlp_in, d_mlp_out = d_mlp_in + grad_in, d_mlp_out + grad_out
-            d_mlp_in_bias = d_mlp_in_bias + d_bias[0]
-        else:
-            d_normed_two = dx.astype(f32)
-            d_mlp_in, d_mlp_out, d_mlp_in_bias = grad_in, grad_out, d_bias[0]
-    d_mlp_in, d_mlp_out = lax.psum((d_mlp_in.astype(bf16), d_mlp_out.astype(bf16)), "batch")
-
+        kept = (hidden, d_pre)
+        d_mlp_in_bias = d_mlp_in_bias + d_bias[0]
+        returned_dx.append(rotated(dx, "mlp", -by))
+        returned_y.append(y)
+    hidden, d_pre, d_bias, y_own, dx_own = mlp_block(
+        normed_two, cotangent, 0, mlp_in, bias_rows, mlp_out, n_mlp * L, 0, kept
+    )
+    d_mlp_in_bias = d_mlp_in_bias + d_bias[0]
+    over_rows = lambda a, b: lax.dot_general(
+        a, b, (((0,), (0,)), ((), ())), preferred_element_type=f32
+    )
+    all_rows = jnp.concatenate(
+        [normed_two] + [piece for pair in zip(arrived_lo, arrived_hi) for piece in pair], axis=0
+    )
+    d_mlp_in = over_rows(all_rows, d_pre).astype(bf16)
+    d_mlp_out = over_rows(hidden, jnp.concatenate(cotangents, axis=0)).astype(bf16)
+
+    batch_bits, mlp_bits = axis_bits("batch"), axis_bits("mlp")
+    core, near, far = batch_bits[:1], batch_bits[1:2], batch_bits[2:]
+    d_mlp_in = scatter_sum(d_mlp_in, core)
+    d_mlp_out = scatter_sum(d_mlp_out, core)
+
+    returned_dx, returned_y = lax.optimization_barrier((returned_dx, returned_y))
+    returned_y = [rotated(y, "mlp", -by) for (by, part), y in zip(calls, returned_y)]
+    halves = [dx_own[:HALF].astype(f32), dx_own[HALF:].astype(f32)]
+    for (by, part), dx in zip(calls, returned_dx):
+        halves[part] = halves[part] + dx.astype(f32)
+    d_normed_two = jnp.concatenate(halves, axis=0)
     upstream = cotangent.astype(f32)
     d_out_bias = jnp.sum(upstream, axis=0)
     d_middle_norm, d_ln2_gain, d_ln2_bias = norm_backward(middle, gain_two, bias_two, d_normed_two)
     d_middle = upstream + d_middle_norm
     d_branch = d_middle.astype(bf16)
     d_attn_out_bias = jnp.sum(d_branch, axis=0, dtype=f32)
-    d_qkv, d_tail, sums = attention_backward(
-        doc_lengths, qkv, mem_k, mem_v, d_branch, attn_out, lse_local, lse_mem, basis_t
-    )
-    over_rows = (((0,), (0,)), ((), ()))
-    grads = [
-        lax.dot_general(normed, d_qkv[0], over_rows, preferred_element_type=f32),
-        lax.dot_general(normed, d_qkv[1], over_rows, preferred_element_type=f32)
-        + lax.dot_general(normed_tail, d_tail[0], over_rows, preferred_element_type=f32),
-        lax.dot_general(normed, d_qkv[2], over_rows, preferred_element_type=f32)
-        + lax.dot_general(normed_tail, d_tail[1], over_rows, preferred_element_type=f32),
-        lax.dot_general(mixture, d_branch, over_rows, preferred_element_type=f32),
-    ]
-    summed = sum_rows(jnp.concatenate([grad.astype(bf16) for grad in grads], axis=0))
-
+    d_branch, d_mlp_in, d_mlp_out = lax.optimization_barrier((d_branch, d_mlp_in, d_mlp_out))
+
+    in_steps, out_steps = near + far, far + near
+    d_mlp_in = scatter_sum(d_mlp_in, in_steps)
+    d_mlp_out = scatter_sum(d_mlp_out, out_steps)
+
+    backward = lambda first, pairs, d: attention_backward(
+        first, pairs, doc_lengths, qkv, mem_k, mem_v, d, attn_out, lse_local, lse_mem, basis_t
+    )
+    early = PAIRS // 3
+    d_one, d_tail_one, sums_one = backward(0, early, d_branch)
+    d_attn_out = over_rows(mixture, d_branch)
+
+    def weight_grads(d, d_tail):
+        return [
+            over_rows(normed, d[0]),
+            over_rows(normed, d[1]) + over_rows(normed_tail, d_tail[0]),
+            over_rows(normed, d[2]) + over_rows(normed_tail, d_tail[1]),
+        ]
+
+    join = lambda pieces: jnp.concatenate([piece.astype(bf16) for piece in pieces], axis=1)
+    grads_one = scatter_sum(join(weight_grads(d_one, d_tail_one) + [d_attn_out]), core)
+    d_branch, grads_one = lax.optimization_barrier((d_branch, grads_one))
+    d_two, d_tail_two, sums_two = backward(early, PAIRS - early, d_branch)
+    d_two, returned_y = lax.optimization_barrier((d_two, returned_y))
+    one_steps, two_steps = mlp_bits + near + far, near + mlp_bits + far
+    grads_one = scatter_sum(grads_one, one_steps)
+    grads_two = scatter_sum(join(weight_grads(d_two, d_tail_two)), core + two_steps)
+
+    d_qkv = jnp.concatenate([d_one, d_two], axis=2)
+    d_tail = jnp.concatenate([d_tail_one, d_tail_two], axis=2)
+    sums = jnp.concatenate([sums_one, sums_two], axis=1)
     columns = [attn_in[:, i * D : (i + 1) * D] for i in range(3)]
     d_tail_rows = dot_nt(d_tail[0], columns[1]) + dot_nt(d_tail[1], columns[2])
     from_next = rotated(d_tail_rows.astype(bf16), "mlp", -1)
     d_normed = (
         dot_nt(d_qkv[0], columns[0]) + dot_nt(d_qkv[1], columns[1]) + dot_nt(d_qkv[2], columns[2])
     )
-    d_normed = jnp.concatenate(
-        [d_normed[:HALF], d_normed[HALF:] + from_next.astype(f32)], axis=0
-    )
-    d_in_norm, d_ln1_gain, d_ln1_bias = norm_backward(activations, gain_one, bias_one, d_normed)
-    input_grad = (d_middle + d_in_norm).astype(bf16)
-
-    result = partial_results[0].astype(f32)
-    for by in range(1, n_mlp):
-        result = result + rotated(partial_results[by], "mlp", -by).astype(f32)
-    layer_output = (middle + (result + mlp_out_bias)).astype(bf16)
+    unused, d_ln1_gain, d_ln1_bias = norm_backward(activations, gain_one, bias_one, d_normed)
+    unused, d_tail_gain, d_tail_bias = norm_backward(tail_rows, gain_one, bias_one, d_tail_rows)
+    d_ln1_gain, d_ln1_bias = d_ln1_gain + d_tail_gain, d_ln1_bias + d_tail_bias
 
     hidden_count = mlp_in.shape[1]
     placed_bias = lax.dynamic_update_slice(
@@ -624,7 +730,36 @@
         axis=0,
     )
     vectors = sum_small(vectors)
-    d_attn_in = jnp.concatenate([summed[i * D : (i + 1) * D] for i in range(3)], axis=1)
+
+    d_normed = jnp.concatenate(
+        [d_normed[:HALF], d_normed[HALF:] + from_next.astype(f32)], axis=0
+    )
+    d_in_norm, unused, unused = norm_backward(activations, gain_one, bias_one, d_normed)
+    input_grad = (d_middle + d_in_norm).astype(bf16)
+
+    halves = [y_own[:HALF].astype(f32), y_own[HALF:].astype(f32)]
+    for (by, part), y in zip(calls, returned_y):
+        halves[part] = halves[part] + y.astype(f32)
+    result = jnp.concatenate(halves, axis=0)
+    layer_output = (middle + (result + mlp_out_bias)).astype(bf16)
+
+    d_mlp_in = gather(d_mlp_in, core + in_steps)
+    d_mlp_out = gather(d_mlp_out, core + out_steps)
+    grads_one = gather(grads_one, core + one_steps)
+    grads_two = gather(grads_two, core + two_steps)
+    width = early * LANES
+    rest = D - width
+    d_attn_in = jnp.concatenate(
+        [
+            piece
+            for i in range(3)
+            for piece in (
+                grads_one[:, i * width : (i + 1) * width],
+                grads_two[:, i * rest : (i + 1) * rest],
+            )
+        ],
+        axis=1,
+    )
     return (
         layer_output,
         input_grad,
@@ -632,7 +767,7 @@
         vectors[1],
         d_attn_in.astype(f32),
         vectors[6:8],
-        summed[3 * D :].astype(f32),
+        grads_one[:, 3 * width :].astype(f32),
         vectors[2],
         vectors[3],
         vectors[4],

time: 375 us -> 344 us (0.917)
  waiting for transfers between devices: 154 us -> 106 us
  between operations: 15.1 us -> 2.26 us
  local copies, waits for them, and re-layouts: 16.2 us -> 28.9 us
  starting transfers between devices: 36.3 us -> 44.6 us
  Pallas kernels: 74.9 us -> 82.2 us
  other arithmetic: 40.6 us -> 47.5 us
  matrix products: 33.6 us -> 28.6 us
    psum x1 -> x0, waiting for transfers between devices: 47.5 us -> none  [shards(): lax.psum((d_mlp_in.astype(bf16), d_mlp_out.astype(bf16)), 'batch')]
    ppermute x6 -> x9, waiting for transfers between devices: 44.4 us -> 5.72 us  [rotated(): lax.ppermute(value, axis, [(i, (i + by) % count) for i in range(count)])]
    ppermute x19 -> x41, waiting for transfers between devices: 62.4 us -> 99.9 us  [swapped(): return lax.ppermute(value, axis, [(i, i ^ 1 << bit) for i in range(count)])]
    ppermute x19 -> x41, starting transfers between devices: 27.6 us -> 35.1 us  [swapped(): return lax.ppermute(value, axis, [(i, i ^ 1 << bit) for i in range(count)])]
    pallas_call x3 -> x5, Pallas kernels: 49.4 us -> 56.9 us  [the longest x3 30.1 us: mlp_block(): pl.pallas_call(mlp_kernel, grid=(hidden // tile,), in_specs=[fixed, pl.Bl...]
    unnamed x92 -> x98, local copies, waits for them, and re-layouts: 4.87 us -> 9.01 us
    convert_element_type x7 -> x18, other arithmetic: 7.95 us -> 11.3 us  [halve(): return (kept.astype(f32) + got.astype(f32)).astype(value.dtype)]
    dot_general x10 -> x13, matrix products: 19.7 us -> 16.6 us  [shards(): lax.dot_general(a, b, (((0,), (0,)), ((), ())), preferred_element_type=f32)]
  transfers between devices with their start and end apart: 26 -> 50, of which waited for: 20 -> 25; matrix products, arithmetic and copies ran while one was open for 15% -> 27% of each run, Pallas kernels for 10% -> 24%
where the time goes in v2:
time: 344 us; the launch traced here: 340 us
  waiting for transfers between devices  106 us (31%)
  Pallas kernels  82.2 us (24%)
  other arithmetic  47.5 us (14%)
  starting transfers between devices  44.6 us (13%)
  local copies, waits for them, and re-layouts  28.9 us (8%)
  matrix products  28.6 us (8%)
    ppermute x41, waiting for transfers between devices, swapped(): return lax.ppermute(value, axis, [(i, i ^ 1 << bit) for i in range(count)])  99.9 us
    ppermute x41, starting transfers between devices, swapped(): return lax.ppermute(value, axis, [(i, i ^ 1 << bit) for i in range(count)])  35.1 us
    pallas_call x3, Pallas kernels, mlp_block(): pl.pallas_call(mlp_kernel, grid=(hidden // tile,), in_specs=[fixed, pl.Bl...  30.1 us
    pallas_call x2, Pallas kernels, attention_backward(): pl.pallas_call(backward_kernel, grid=(pairs,), in_specs=[pl.BlockSpec(mem...  26.8 us
    dot_general x13, matrix products, shards(): lax.dot_general(a, b, (((0,), (0,)), ((), ())), preferred_element_type=f32)  16.6 us
    pallas_call x1, Pallas kernels, local_attention(): pl.pallas_call(local_kernel, grid=(PAIRS,), in_specs=[pl.BlockSpec(memory...  13.3 us
    pallas_call x1, Pallas kernels, memory_attention(): pl.pallas_call(memory_kernel, grid=(PAIRS,), in_specs=[pl.BlockSpec(memor...  12 us
    convert_element_type x18, other arithmetic, halve(): return (kept.astype(f32) + got.astype(f32)).astype(value.dtype)  11.3 us
  transfers between devices with their start and end apart: 50, of which 25 were waited for; matrix products, arithmetic and copies ran while one was open for 27% of the time, Pallas kernels for 24%

profile of v2, /device:TPU:0, one launch (start us, length us, event | category | flops | bytes accessed | tf_op | source)
XLA Modules:
  0.0 339.6 jit_solution(6562857941059828647)
XLA Ops:
  3.9 3.1 collective-permute-start
  8.1 3.4 %fusion.q_ref.k_ref.v_ref = bf16[512,2304]{1,0:T(8,128)(2,1)} fusion(bf16[512,768]{1,0:T(8,128)(2,1)S(1)} %fusion.9, bf16[768,2304]{1,0:T(8,128)(2,1)S(1)} %copy-done.24, f32[2304]{0:T(1024)S(1)} %pad_maximum_fusion.19), kind=kOutput, calls=%fused_computation.1 | convolution fusion | flops 1814298624 | bytes 6693888 | tf_op jit(solution)/shard_map/dot_general | solution.py:29
  12.2 13.3 %local_attention.1 = (f32[256,768]{1,0:T(8,128)}, f32[6,8,512]{2,1,0:T(8,128)}, bf16[512,768]{1,0:T(8,128)(2,1)}, f32[512,768]{1,0:T(8,128)}, bf16[512,768]{1,0:T(8,128)(2,1)}) custom-call(s32[1,3]{1,0:T(1,128)} %lens.5, bf16[512,2304]{1,0:T(8,128)(2,1)} %fusion.q_ref.k_ref.v_ref, bf16[512,2304]{1,0:T(8,128)(2,1)} %fusion.q_ref.k_ref.v_ref, ...), custom_call_target="tpu_custom_call" | custom-call | flops 2415919104 | bytes 3145728 | tf_op jit(solution)/shard_map/local_attention/pallas_call | solution.py:120
  27.3 2.0 collective-permute-start.2
  31.0 3.4 %convolution_convert_fusion.2.kt_ref.vt_ref = bf16[256,1536]{1,0:T(8,128)(2,1)} fusion(bf16[768,2304]{1,0:T(8,128)(2,1)} %param.19, f32[768]{0:T(1024)S(1)} %convert_element_type.297, f32[768]{0:T(1024)S(1)} %convert_element_type.296, f32[256]{0:T(256)S(1)} %add_rsqrt_fusion, f32[256]{0:T(256)S(1)} %broadcast_multiply_fusion.2, ...), kind=kOutput, calls=%fused_computation.8 | convolution fusion | flops 605552640 | bytes 3549184 | tf_op jit(solution)/shard_map/dot_general | solution.py:29
  35.0 12.0 %memory_attention.1 = (bf16[512,768]{1,0:T(8,128)(2,1)}, bf16[512,768]{1,0:T(8,128)(2,1)}, bf16[512,768]{1,0:T(8,128)(2,1)}, f32[6,8,256]{2,1,0:T(8,128)}, f32[5...) custom-call(s32[1,1]{1,0:T(1,128)S(6)} %select_n.285.reads, ...), custom_call_target="tpu_custom_call", output_to_operand_aliasing={{0}: (10, {}), {4}: (11, {}), {5}: (12, {})} | custom-call | flops 3221225472 | bytes 6291456 | tf_op jit(solution)/shard_map/memory_attention/pallas_call | solution.py:234
  50.9 5.5 %collective-permute-done.2.ct_ref = bf16[512,768]{1,0:T(8,128)(2,1)} collective-permute-done((bf16[512,768]{1,0:T(8,128)(2,1)}, bf16[512,768]{1,0:T(8,128)(2,1)}, u32[]{:S(2)}, u32[]{:S(2)}) %collective-permute-start.2) | collective-permute-done | bytes 786464 | tf_op jit(solution)/shard_map/ppermute | solution.py:511
  57.1 8.8 %mlp_block.3 = (bf16[1024,1536]{1,0:T(8,128)(2,1)}, bf16[1024,1536]{1,0:T(8,128)(2,1)}, f32[8,1536]{1,0:T(8,128)}, bf16[256,768]{1,0:T(8,128)(2,1)}, bf16[256,768]{1,0:T(8,128)(2,1)}) custom-call(bf16[256,768]{1,0:T(8,128)(2,1)} %collective-permute-done.3.x_ref, bf16[512,768]{1,0:T(8,128)(2,1)} %collective-permute-done.2.ct_ref, bf16[768,1536]{1,0:T(8,128)(2,1)} %wi_ref.5, ...), custom_call_target="tpu_custom_call" | custom-call | flops 2415919104 | bytes 7864320 | tf_op jit(solution)/shard_map/mlp_block/pallas_call | solution.py:342
  66.7 8.7 %mlp_block.4 = (bf16[1024,1536]{1,0:T(8,128)(2,1)}, bf16[1024,1536]{1,0:T(8,128)(2,1)}, f32[8,1536]{1,0:T(8,128)}, bf16[256,768]{1,0:T(8,128)(2,1)}, bf16[256,768]{1,0:T(8,128)(2,1)}) custom-call(bf16[256,768]{1,0:T(8,128)(2,1)} %copy-done.22, bf16[512,768]{1,0:T(8,128)(2,1)} %collective-permute-done.2.ct_ref, ...), custom_call_target="tpu_custom_call", output_to_operand_aliasing={{0}: (5, {}), {1}: (6, {})} | custom-call | flops 2415919104 | bytes 7864320 | tf_op jit(solution)/shard_map/mlp_block/pallas_call | solution.py:342
  75.4 2.1 collective-permute-start.5
  77.5 12.6 %mlp_block.5 = (bf16[1024,1536]{1,0:T(8,128)(2,1)}, bf16[1024,1536]{1,0:T(8,128)(2,1)}, f32[8,1536]{1,0:T(8,128)}, bf16[512,768]{1,0:T(8,128)(2,1)}, bf16[512,768]{1,0:T(8,128)(2,1)}) custom-call(bf16[512,768]{1,0:T(8,128)(2,1)} %get-tuple-element.64.x_ref, bf16[512,768]{1,0:T(8,128)(2,1)} %ct_ref.1, ...), custom_call_target="tpu_custom_call", output_to_operand_aliasing={{0}: (5, {}), {1}: (6, {})} | custom-call | flops 4831838208 | bytes 11010048 | tf_op jit(solution)/shard_map/mlp_block/pallas_call | solution.py:342
  90.1 5.0 %convolution_convert_fusion.1 = bf16[768,1536]{1,0:T(8,128)(2,1)S(1)} fusion(bf16[1024,1536]{1,0:T(8,128)(2,1)} %get-tuple-element.79, bf16[256,768]{1,0:T(8,128)(2,1)} %collective-permute-done.3.x_ref, bf16[256,768]{1,0:T(8,128)(2,1)S(1)} %copy-done.23, bf16[512,768]{1,0:T(8,128)(2,1)} %get-tuple-element.64.x_ref), kind=kOutput, calls=%fused_computation.3 | convolution fusion | flops 2421817344 | bytes 7077888 | tf_op jit(solution)/shard_map/dot_general | solution.py:650
  96.4 4.7 %convolution_convert_fusion = bf16[1536,768]{1,0:T(8,128)(2,1)S(1)} fusion(bf16[1024,1536]{1,0:T(8,128)(2,1)S(1)} %copy-done.12, bf16[512,768]{1,0:T(8,128)(2,1)} %collective-permute-done.2.ct_ref, bf16[512,768]{1,0:T(8,128)(2,1)} %ct_ref.1), kind=kOutput, calls=%fused_computation.2 | convolution fusion | flops 2420244480 | bytes 7077888 | tf_op jit(solution)/shard_map/dot_general | solution.py:650
  107.7 2.0 collective-permute-start.10
  109.7 2.5 convert_reduce_fusion.2
  113.9 2.7 add_convert_fusion.3
  116.6 2.6 add_convert_fusion.2
  119.3 9.7 %attention_backward.2 = (bf16[3,512,256]{2,1,0:T(8,128)(2,1)}, bf16[2,256,256]{2,1,0:T(8,128)(2,1)}, f32[8,256]{1,0:T(8,128)}) custom-call(s32[1,3]{1,0:T(1,128)} %lens.5, bf16[512,2304]{1,0:T(8,128)(2,1)} %fusion.q_ref.k_ref.v_ref, bf16[512,2304]{1,0:T(8,128)(2,1)} %fusion.q_ref.k_ref.v_ref, bf16[512,2304]{1,0:T(8,128)(2,1)} %fusion.q_ref.k_ref.v_ref, ...), custom_call_target="tpu_custom_call" | custom-call | flops 3758096384 | bytes 2621440 | tf_op jit(solution)/shard_map/attention_backward/pallas_call | solution.py:468
  140.5 7.4 %collective-permute-done.36 = bf16[192,1536]{1,0:T(8,128)(2,1)S(1)} collective-permute-done((bf16[192,1536]{1,0:T(8,128)(2,1)S(1)}, bf16[192,1536]{1,0:T(8,128)(2,1)S(1)}, u32[]{:S(2)}, u32[]{:S(2)}) %collective-permute-start.36) | collective-permute-done | bytes 589856 | tf_op jit(solution)/shard_map/ppermute | solution.py:516
  149.7 3.7 %collective-permute-done.43 = bf16[384,768]{1,0:T(8,128)(2,1)S(1)} collective-permute-done((bf16[384,768]{1,0:T(8,128)(2,1)S(1)}, bf16[384,768]{1,0:T(8,128)(2,1)S(1)}, u32[]{:S(2)}, u32[]{:S(2)}) %collective-permute-start.43) | collective-permute-done | bytes 589856 | tf_op jit(solution)/shard_map/ppermute | solution.py:516
  153.6 2.7 collective-permute-start.44
  156.2 7.2 %collective-permute-done.37 = bf16[96,1536]{1,0:T(8,128)(2,1)S(1)} collective-permute-done((bf16[96,1536]{1,0:T(8,128)(2,1)S(1)}, bf16[96,1536]{1,0:T(8,128)(2,1)S(1)}, u32[]{:S(2)}, u32[]{:S(2)}) %collective-permute-start.37) | collective-permute-done | bytes 294944 | tf_op jit(solution)/shard_map/ppermute | solution.py:516
  163.8 7.9 %collective-permute-done.44 = bf16[192,768]{1,0:T(8,128)(2,1)S(1)} collective-permute-done((bf16[192,768]{1,0:T(8,128)(2,1)S(1)}, bf16[192,768]{1,0:T(8,128)(2,1)S(1)}, u32[]{:S(2)}, u32[]{:S(2)}) %collective-permute-start.44) | collective-permute-done | bytes 294944 | tf_op jit(solution)/shard_map/ppermute | solution.py:516
  174.6 3.1 collective-permute-done.45
  179.7 17.1 %attention_backward.3 = (bf16[3,512,512]{2,1,0:T(8,128)(2,1)}, bf16[2,256,512]{2,1,0:T(8,128)(2,1)}, f32[8,512]{1,0:T(8,128)}) custom-call(s32[1,3]{1,0:T(1,128)} %lens.5, bf16[512,2304]{1,0:T(8,128)(2,1)} %fusion.q_ref.k_ref.v_ref, bf16[512,2304]{1,0:T(8,128)(2,1)} %fusion.q_ref.k_ref.v_ref, bf16[512,2304]{1,0:T(8,128)(2,1)} %fusion.q_ref.k_ref.v_ref, ...), custom_call_target="tpu_custom_call" | custom-call | flops 7516192768 | bytes 5242880 | tf_op jit(solution)/shard_map/attention_backward/pallas_call | solution.py:468
  196.8 2.8 constant_dynamic-update-slice_fusion
  199.7 2.5 fusion.26
  221.0 2.8 convert_reduce_fusion
  224.0 3.5 %collective-permute-start.47 = (bf16[192,768]{1,0:T(8,128)(2,1)S(1)}, bf16[192,768]{1,0:T(8,128)(2,1)S(1)}, u32[]{:S(2)}, u32[]{:S(2)}) collective-permute-start(bf16[192,768]{1,0:T(8,128)(2,1)S(1)} %pad_maximum_fusion.16), channel_id=1, source_target_pairs={{0,16},{2,18},{4,20},{6,22},{8,24},{10,26},{12,28},{14,30},{16,0},... | collective-permute-start | bytes 884744 | tf_op jit(solution)/shard_map/ppermute | solution.py:516
  229.1 2.5 collective-permute-done.13
  234.2 6.6 %collective-permute-done.14 = f32[12,768]{1,0:T(8,128)S(1)} collective-permute-done((f32[12,768]{1,0:T(8,128)S(1)}, f32[12,768]{1,0:T(8,128)S(1)}, u32[]{:S(2)}, u32[]{:S(2)}) %collective-permute-start.14) | collective-permute-done | bytes 36896 | tf_op jit(solution)/shard_map/ppermute | solution.py:516
  247.5 2.6 collective-permute-done.16
  256.0 5.3 %collective-permute-done.48 = bf16[384,768]{1,0:T(8,128)(2,1)S(1)} collective-permute-done((bf16[384,768]{1,0:T(8,128)(2,1)}, bf16[384,768]{1,0:T(8,128)(2,1)S(1)}, u32[]{:S(2)}, u32[]{:S(2)}) %collective-permute-start.48) | collective-permute-done | bytes 589856 | tf_op jit(solution)/shard_map/ppermute | solution.py:516
  263.7 7.3 %collective-permute-done.20 = bf16[24,1536]{1,0:T(8,128)(2,1)S(1)} collective-permute-done((bf16[24,1536]{1,0:T(8,128)(2,1)S(1)}, bf16[24,1536]{1,0:T(8,128)(2,1)S(1)}, u32[]{:S(2)}, u32[]{:S(2)}) %collective-permute-start.20) | collective-permute-done | bytes 73760 | tf_op jit(solution)/shard_map/ppermute | solution.py:516
  273.8 2.6 collective-permute-done.21
  276.5 7.3 %collective-permute-done.27 = bf16[192,1536]{1,0:T(8,128)(2,1)S(1)} collective-permute-done((bf16[192,1536]{1,0:T(8,128)(2,1)S(1)}, bf16[192,1536]{1,0:T(8,128)(2,1)S(1)}, u32[]{:S(2)}, u32[]{:S(2)}) %collective-permute-start.27) | collective-permute-done | bytes 589856 | tf_op jit(solution)/shard_map/ppermute | solution.py:516
  285.5 5.3 %collective-permute-done.28 = bf16[96,1536]{1,0:T(8,128)(2,1)S(1)} collective-permute-done((bf16[96,1536]{1,0:T(8,128)(2,1)S(1)}, bf16[96,1536]{1,0:T(8,128)(2,1)S(1)}, u32[]{:S(2)}, u32[]{:S(2)}) %collective-permute-start.28) | collective-permute-done | bytes 294944 | tf_op jit(solution)/shard_map/ppermute | solution.py:516
  293.0 3.4 collective-permute-done.29
  296.4 2.2 collective-permute-start.30
  298.7 3.8 %collective-permute-done.30 = bf16[24,1536]{1,0:T(8,128)(2,1)S(1)} collective-permute-done((bf16[24,1536]{1,0:T(8,128)(2,1)S(1)}, bf16[24,1536]{1,0:T(8,128)(2,1)S(1)}, u32[]{:S(2)}, u32[]{:S(2)}) %collective-permute-start.30) | collective-permute-done | bytes 73760 | tf_op jit(solution)/shard_map/ppermute | solution.py:516
  302.6 2.2 collective-permute-start.31
  306.0 2.1 collective-permute-done.31
  308.6 4.7 %collective-permute-done.32 = bf16[48,1536]{1,0:T(8,128)(2,1)S(1)} collective-permute-done((bf16[48,1536]{1,0:T(8,128)(2,1)S(1)}, bf16[48,1536]{1,0:T(8,128)(2,1)S(1)}, u32[]{:S(2)}, u32[]{:S(2)}) %collective-permute-start.32) | collective-permute-done | bytes 147488 | tf_op jit(solution)/shard_map/ppermute | solution.py:516
  314.8 2.8 maximum_convert_fusion
  317.6 2.5 collective-permute-done.33
  322.2 8.1 %collective-permute-done.34 = bf16[192,1536]{1,0:T(8,128)(2,1)S(1)} collective-permute-done((bf16[192,1536]{1,0:T(8,128)(2,1)S(1)}, bf16[192,1536]{1,0:T(8,128)(2,1)S(1)}, u32[]{:S(2)}, u32[]{:S(2)}) %collective-permute-start.34) | collective-permute-done | bytes 589856 | tf_op jit(solution)/shard_map/ppermute | solution.py:516
  330.6 2.5 maximum_convert_fusion.1
  335.9 3.5 %convert_element_type.370 = f32[768,2304]{1,0:T(8,128)} convert(bf16[768,2304]{1,0:T(8,128)(2,1)S(1)} %fusion.47) | non-fusion elementwise | flops 1769472 | bytes 10616832 | tf_op jit(solution)/shard_map/convert_element_type | solution.py:768
  (333 shorter events, 95.2 us)
Async XLA Ops:
  3.9 26.1 %collective-permute-start = (bf16[272,768]{1,0:T(8,128)(2,1)S(1)}, bf16[272,768]{1,0:T(8,128)(2,1)S(1)}, u32[]{:S(2)}, u32[]{:S(2)}) collective-permute-start(bf16[272,768]{1,0:T(8,128)(2,1)S(1)} %concatenate.99), channel_id=1, source_target_pairs={{0,1},{1,0},{2,3},{3,2},{4,5},{5,4},{6,7},{7,6},{8,9},{9,8},{10,11... | collective-permute-start | bytes 1253384 | tf_op jit(solution)/shard_map/ppermute | solution.py:511
  27.3 23.6 %collective-permute-start.3 = (bf16[256,768]{1,0:T(8,128)(2,1)}, bf16[256,768]{1,0:T(8,128)(2,1)}, u32[]{:S(2)}, u32[]{:S(2)}) collective-permute-start(bf16[256,768]{1,0:T(8,128)(2,1)} %slice.170), channel_id=1, source_target_pairs={{0,1},{1,0},{2,3},{3,2},{4,5},{5,4},{6,7},{7,6},{8,9},{9,8},{10,11... | collective-permute-start | bytes 1179656 | tf_op jit(solution)/shard_map/ppermute | solution.py:511
  27.3 29.1 %collective-permute-start.2 = (bf16[512,768]{1,0:T(8,128)(2,1)}, bf16[512,768]{1,0:T(8,128)(2,1)}, u32[]{:S(2)}, u32[]{:S(2)}) collective-permute-start(bf16[512,768]{1,0:T(8,128)(2,1)} %ct_ref.1), channel_id=1, source_target_pairs={{0,1},{1,0},{2,3},{3,2},{4,5},{5,4},{6,7},{7,6},{8,9},{9,8},{10,11... | collective-permute-start | bytes 2359304 | tf_op jit(solution)/shard_map/ppermute | solution.py:511
  48.9 17.0 %collective-permute-start.1 = (bf16[256,768]{1,0:T(8,128)(2,1)}, bf16[256,768]{1,0:T(8,128)(2,1)S(1)}, u32[]{:S(2)}, u32[]{:S(2)}) collective-permute-start(bf16[256,768]{1,0:T(8,128)(2,1)} %slice.169), channel_id=1, source_target_pairs={{0,1},{1,0},{2,3},{3,2},{4,5},{5,4},{6,7},{7,6},{8,9},{9,8},{10,11... | collective-permute-start | bytes 1179656 | tf_op jit(solution)/shard_map/ppermute | solution.py:511
  65.8 38.8 %collective-permute-start.4 = (bf16[256,768]{1,0:T(8,128)(2,1)}, bf16[256,768]{1,0:T(8,128)(2,1)}, u32[]{:S(2)}, u32[]{:S(2)}) collective-permute-start(bf16[256,768]{1,0:T(8,128)(2,1)} %get-tuple-element.73), channel_id=1, source_target_pairs={{0,1},{1,0},{2,3},{3,2},{4,5},{5,4},{6,7},{7,6},{8,9},{9,8},{10,11... | collective-permute-start | bytes 1179656 | tf_op jit(solution)/shard_map/ppermute | solution.py:511
  75.4 29.3 %collective-permute-start.5 = (bf16[256,768]{1,0:T(8,128)(2,1)}, bf16[256,768]{1,0:T(8,128)(2,1)}, u32[]{:S(2)}, u32[]{:S(2)}) collective-permute-start(bf16[256,768]{1,0:T(8,128)(2,1)} %get-tuple-element.74), channel_id=1, source_target_pairs={{0,1},{1,0},{2,3},{3,2},{4,5},{5,4},{6,7},{7,6},{8,9},{9,8},{10,11... | collective-permute-start | bytes 1179656 | tf_op jit(solution)/shard_map/ppermute | solution.py:511
  96.4 17.5 %collective-permute-start.6 = (bf16[384,1536]{1,0:T(8,128)(2,1)}, bf16[384,1536]{1,0:T(8,128)(2,1)}, u32[]{:S(2)}, u32[]{:S(2)}) collective-permute-start(bf16[384,1536]{1,0:T(8,128)(2,1)} %constant_dynamic-slice_fusion.17), channel_id=1, source_target_pairs={{0,2},{2,0},{4,6},{6,4},{8,10},{10,8},{12,14},{14,12},{16,18},{18,... | collective-permute-start | bytes 3538952 | tf_op jit(solution)/shard_map/ppermute | solution.py:516
  102.9 13.7 %collective-permute-start.7 = (bf16[768,768]{1,0:T(8,128)(2,1)}, bf16[768,768]{1,0:T(8,128)(2,1)}, u32[]{:S(2)}, u32[]{:S(2)}) collective-permute-start(bf16[768,768]{1,0:T(8,128)(2,1)} %constant_dynamic-slice_fusion.16), channel_id=1, source_target_pairs={{0,2},{2,0},{4,6},{6,4},{8,10},{10,8},{12,14},{14,12},{16,18},{18,... | collective-permute-start | bytes 3538952 | tf_op jit(solution)/shard_map/ppermute | solution.py:516
  107.6 89.2 %collective-permute-start.9 = (bf16[256,768]{1,0:T(8,128)(2,1)}, bf16[256,768]{1,0:T(8,128)(2,1)S(1)}, u32[]{:S(2)}, u32[]{:S(2)}) collective-permute-start(bf16[256,768]{1,0:T(8,128)(2,1)} %get-tuple-element.90), channel_id=1, source_target_pairs={{0,1},{1,0},{2,3},{3,2},{4,5},{5,4},{6,7},{7,6},{8,9},{9,8},{10,11... | collective-permute-start | bytes 1179656 | tf_op jit(solution)/shard_map/ppermute | solution.py:511
  107.7 89.2 %collective-permute-start.10 = (bf16[256,768]{1,0:T(8,128)(2,1)}, bf16[256,768]{1,0:T(8,128)(2,1)}, u32[]{:S(2)}, u32[]{:S(2)}) collective-permute-start(bf16[256,768]{1,0:T(8,128)(2,1)} %get-tuple-element.91), channel_id=1, source_target_pairs={{0,1},{1,0},{2,3},{3,2},{4,5},{5,4},{6,7},{7,6},{8,9},{9,8},{10,11... | collective-permute-start | bytes 1179656 | tf_op jit(solution)/shard_map/ppermute | solution.py:511
  133.1 14.7 %collective-permute-start.36 = (bf16[192,1536]{1,0:T(8,128)(2,1)S(1)}, bf16[192,1536]{1,0:T(8,128)(2,1)S(1)}, u32[]{:S(2)}, u32[]{:S(2)}) collective-permute-start(bf16[192,1536]{1,0:T(8,128)(2,1)S(1)} %constant_dynamic-slice_fusion.5), channel_id=1, source_target_pairs={{0,4},{2,6},{4,0},{6,2},{8,12},{10,14},{12,8},{14,10},{16,20},{18,... | collective-permute-start | bytes 1769480 | tf_op jit(solution)/shard_map/ppermute | solution.py:516
  135.9 42.5 %collective-permute-start.8 = (bf16[384,1536]{1,0:T(8,128)(2,1)S(1)}, bf16[384,1536]{1,0:T(8,128)(2,1)S(1)}, u32[]{:S(2)}, u32[]{:S(2)}) collective-permute-start(bf16[384,1536]{1,0:T(8,128)(2,1)S(1)} %constant_dynamic-slice_fusion.15), channel_id=1, source_target_pairs={{0,2},{2,0},{4,6},{6,4},{8,10},{10,8},{12,14},{14,12},{16,18},{18,... | collective-permute-start | bytes 3538952 | tf_op jit(solution)/shard_map/ppermute | solution.py:516
  137.1 16.3 %collective-permute-start.43 = (bf16[384,768]{1,0:T(8,128)(2,1)S(1)}, bf16[384,768]{1,0:T(8,128)(2,1)S(1)}, u32[]{:S(2)}, u32[]{:S(2)}) collective-permute-start(bf16[384,768]{1,0:T(8,128)(2,1)S(1)} %constant_dynamic-slice_fusion.2), channel_id=1, source_target_pairs={{0,8},{2,10},{4,12},{6,14},{8,0},{10,2},{12,4},{14,6},{16,24},{18,... | collective-permute-start | bytes 1769480 | tf_op jit(solution)/shard_map/ppermute | solution.py:516
  148.0 15.4 %collective-permute-start.37 = (bf16[96,1536]{1,0:T(8,128)(2,1)S(1)}, bf16[96,1536]{1,0:T(8,128)(2,1)S(1)}, u32[]{:S(2)}, u32[]{:S(2)}) collective-permute-start(bf16[96,1536]{1,0:T(8,128)(2,1)S(1)} %constant_dynamic-slice_fusion.4), channel_id=1, source_target_pairs={{0,8},{2,10},{4,12},{6,14},{8,0},{10,2},{12,4},{14,6},{16,24},{18,... | collective-permute-start | bytes 884744 | tf_op jit(solution)/shard_map/ppermute | solution.py:516
  153.6 18.2 %collective-permute-start.44 = (bf16[192,768]{1,0:T(8,128)(2,1)S(1)}, bf16[192,768]{1,0:T(8,128)(2,1)S(1)}, u32[]{:S(2)}, u32[]{:S(2)}) collective-permute-start(bf16[192,768]{1,0:T(8,128)(2,1)S(1)} %constant_dynamic-slice_fusion.1), channel_id=1, source_target_pairs={{0,16},{2,18},{4,20},{6,22},{8,24},{10,26},{12,28},{14,30},{16,0},... | collective-permute-start | bytes 884744 | tf_op jit(solution)/shard_map/ppermute | solution.py:516
  163.6 10.4 %collective-permute-start.38 = (bf16[48,1536]{1,0:T(8,128)(2,1)S(1)}, bf16[48,1536]{1,0:T(8,128)(2,1)S(1)}, u32[]{:S(2)}, u32[]{:S(2)}) collective-permute-start(bf16[48,1536]{1,0:T(8,128)(2,1)S(1)} %constant_dynamic-slice_fusion.3), channel_id=1, source_target_pairs={{0,16},{2,18},{4,20},{6,22},{8,24},{10,26},{12,28},{14,30},{16,0},... | collective-permute-start | bytes 442376 | tf_op jit(solution)/shard_map/ppermute | solution.py:516
  171.9 5.9 %collective-permute-start.45 = (bf16[96,768]{1,0:T(8,128)(2,1)S(1)}, bf16[96,768]{1,0:T(8,128)(2,1)S(1)}, u32[]{:S(2)}, u32[]{:S(2)}) collective-permute-start(bf16[96,768]{1,0:T(8,128)(2,1)S(1)} %constant_dynamic-slice_fusion), channel_id=1, source_target_pairs={{0,4},{2,6},{4,0},{6,2},{8,12},{10,14},{12,8},{14,10},{16,20},{18,... | collective-permute-start | bytes 442376 | tf_op jit(solution)/shard_map/ppermute | solution.py:516
  174.6 40.9 %collective-permute-start.39 = (bf16[48,1536]{1,0:T(8,128)(2,1)}, bf16[48,1536]{1,0:T(8,128)(2,1)}, u32[]{:S(2)}, u32[]{:S(2)}) collective-permute-start(bf16[48,1536]{1,0:T(8,128)(2,1)} %add_convert_fusion.16), channel_id=1, source_target_pairs={{0,16},{2,18},{4,20},{6,22},{8,24},{10,26},{12,28},{14,30},{16,0},... | collective-permute-start | bytes 442376 | tf_op jit(solution)/shard_map/ppermute | solution.py:516
  177.8 39.3 %collective-permute-start.46 = (bf16[96,768]{1,0:T(8,128)(2,1)S(1)}, bf16[96,768]{1,0:T(8,128)(2,1)}, u32[]{:S(2)}, u32[]{:S(2)}) collective-permute-start(bf16[96,768]{1,0:T(8,128)(2,1)S(1)} %add_convert_fusion.15), channel_id=1, source_target_pairs={{0,4},{2,6},{4,0},{6,2},{8,12},{10,14},{12,8},{14,10},{16,20},{18,... | collective-permute-start | bytes 442376 | tf_op jit(solution)/shard_map/ppermute | solution.py:516
  206.1 12.1 %collective-permute-start.11 = (bf16[256,768]{1,0:T(8,128)(2,1)S(1)}, bf16[256,768]{1,0:T(8,128)(2,1)S(1)}, u32[]{:S(2)}, u32[]{:S(2)}) collective-permute-start(bf16[256,768]{1,0:T(8,128)(2,1)S(1)} %get-tuple-element.147), channel_id=1, source_target_pairs={{0,1},{1,0},{2,3},{3,2},{4,5},{5,4},{6,7},{7,6},{8,9},{9,8},{10,11... | collective-permute-start | bytes 1179656 | tf_op jit(solution)/shard_map/ppermute | solution.py:511
  206.8 34.1 %collective-permute-start.17 = (bf16[192,1536]{1,0:T(8,128)(2,1)S(1)}, bf16[192,1536]{1,0:T(8,128)(2,1)}, u32[]{:S(2)}, u32[]{:S(2)}) collective-permute-start(bf16[192,1536]{1,0:T(8,128)(2,1)S(1)} %constant_dynamic-slice_fusion.14), channel_id=1, source_target_pairs={{0,1},{1,0},{2,3},{3,2},{4,5},{5,4},{6,7},{7,6},{8,9},{9,8},{10,11... | collective-permute-start | bytes 1769480 | tf_op jit(solution)/shard_map/ppermute | solution.py:516
  212.0 59.2 %collective-permute-start.26 = (bf16[384,1536]{1,0:T(8,128)(2,1)}, bf16[384,1536]{1,0:T(8,128)(2,1)}, u32[]{:S(2)}, u32[]{:S(2)}) collective-permute-start(bf16[384,1536]{1,0:T(8,128)(2,1)} %constant_dynamic-slice_fusion.10), channel_id=1, source_target_pairs={{0,2},{2,0},{4,6},{6,4},{8,10},{10,8},{12,14},{14,12},{16,18},{18,... | collective-permute-start | bytes 3538952 | tf_op jit(solution)/shard_map/ppermute | solution.py:516
  216.6 12.5 %collective-permute-start.40 = (bf16[96,1536]{1,0:T(8,128)(2,1)S(1)}, bf16[96,1536]{1,0:T(8,128)(2,1)S(1)}, u32[]{:S(2)}, u32[]{:S(2)}) collective-permute-start(bf16[96,1536]{1,0:T(8,128)(2,1)S(1)} %pad_maximum_fusion.15), channel_id=1, source_target_pairs={{0,8},{2,10},{4,12},{6,14},{8,0},{10,2},{12,4},{14,6},{16,24},{18,... | collective-permute-start | bytes 884744 | tf_op jit(solution)/shard_map/ppermute | solution.py:516
  224.0 20.4 %collective-permute-start.47 = (bf16[192,768]{1,0:T(8,128)(2,1)S(1)}, bf16[192,768]{1,0:T(8,128)(2,1)S(1)}, u32[]{:S(2)}, u32[]{:S(2)}) collective-permute-start(bf16[192,768]{1,0:T(8,128)(2,1)S(1)} %pad_maximum_fusion.16), channel_id=1, source_target_pairs={{0,16},{2,18},{4,20},{6,22},{8,24},{10,26},{12,28},{14,30},{16,0},... | collective-permute-start | bytes 884744 | tf_op jit(solution)/shard_map/ppermute | solution.py:516
  227.5 4.2 %collective-permute-start.13 = (f32[12,768]{1,0:T(8,128)S(1)}, f32[12,768]{1,0:T(8,128)S(1)}, u32[]{:S(2)}, u32[]{:S(2)}) collective-permute-start(f32[12,768]{1,0:T(8,128)S(1)} %add.342), channel_id=1, source_target_pairs={{0,4},{2,6},{4,0},{6,2},{8,12},{10,14},{12,8},{14,10},{16,20},{18,... | collective-permute-start | bytes 110600 | tf_op jit(solution)/shard_map/ppermute | solution.py:516
  231.7 9.2 %collective-permute-start.14 = (f32[12,768]{1,0:T(8,128)S(1)}, f32[12,768]{1,0:T(8,128)S(1)}, u32[]{:S(2)}, u32[]{:S(2)}) collective-permute-start(f32[12,768]{1,0:T(8,128)S(1)} %add.343), channel_id=1, source_target_pairs={{0,8},{2,10},{4,12},{6,14},{8,0},{10,2},{12,4},{14,6},{16,24},{18,... | collective-permute-start | bytes 110600 | tf_op jit(solution)/shard_map/ppermute | solution.py:516
  232.7 22.9 %collective-permute-start.41 = (bf16[192,1536]{1,0:T(8,128)(2,1)}, bf16[192,1536]{1,0:T(8,128)(2,1)S(1)}, u32[]{:S(2)}, u32[]{:S(2)}) collective-permute-start(bf16[192,1536]{1,0:T(8,128)(2,1)} %pad_maximum_fusion.11), channel_id=1, source_target_pairs={{0,4},{2,6},{4,0},{6,2},{8,12},{10,14},{12,8},{14,10},{16,20},{18,... | collective-permute-start | bytes 1769480 | tf_op jit(solution)/shard_map/ppermute | solution.py:516
  240.8 5.0 %collective-permute-start.15 = (f32[12,768]{1,0:T(8,128)S(1)}, f32[12,768]{1,0:T(8,128)S(1)}, u32[]{:S(2)}, u32[]{:S(2)}) collective-permute-start(f32[12,768]{1,0:T(8,128)S(1)} %add.344), channel_id=1, source_target_pairs={{0,16},{2,18},{4,20},{6,22},{8,24},{10,26},{12,28},{14,30},{16,0},... | collective-permute-start | bytes 110600 | tf_op jit(solution)/shard_map/ppermute | solution.py:516
  242.9 10.8 %collective-permute-start.18 = (bf16[96,1536]{1,0:T(8,128)(2,1)}, bf16[96,1536]{1,0:T(8,128)(2,1)S(1)}, u32[]{:S(2)}, u32[]{:S(2)}) collective-permute-start(bf16[96,1536]{1,0:T(8,128)(2,1)} %constant_dynamic-slice_fusion.13), channel_id=1, source_target_pairs={{0,4},{2,6},{4,0},{6,2},{8,12},{10,14},{12,8},{14,10},{16,20},{18,... | collective-permute-start | bytes 884744 | tf_op jit(solution)/shard_map/ppermute | solution.py:516
  247.5 13.8 %collective-permute-start.48 = (bf16[384,768]{1,0:T(8,128)(2,1)}, bf16[384,768]{1,0:T(8,128)(2,1)S(1)}, u32[]{:S(2)}, u32[]{:S(2)}) collective-permute-start(bf16[384,768]{1,0:T(8,128)(2,1)} %pad_maximum_fusion.12), channel_id=1, source_target_pairs={{0,8},{2,10},{4,12},{6,14},{8,0},{10,2},{12,4},{14,6},{16,24},{18,... | collective-permute-start | bytes 1769480 | tf_op jit(solution)/shard_map/ppermute | solution.py:516
  253.8 9.6 %collective-permute-start.19 = (bf16[48,1536]{1,0:T(8,128)(2,1)S(1)}, bf16[48,1536]{1,0:T(8,128)(2,1)S(1)}, u32[]{:S(2)}, u32[]{:S(2)}) collective-permute-start(bf16[48,1536]{1,0:T(8,128)(2,1)S(1)} %constant_dynamic-slice_fusion.12), channel_id=1, source_target_pairs={{0,8},{2,10},{4,12},{6,14},{8,0},{10,2},{12,4},{14,6},{16,24},{18,... | collective-permute-start | bytes 442376 | tf_op jit(solution)/shard_map/ppermute | solution.py:516
  255.9 52.3 %collective-permute-start.42 = (bf16[384,1536]{1,0:T(8,128)(2,1)S(1)}, bf16[384,1536]{1,0:T(8,128)(2,1)S(1)}, u32[]{:S(2)}, u32[]{:S(2)}) collective-permute-start(bf16[384,1536]{1,0:T(8,128)(2,1)S(1)} %pad_maximum_fusion.6), channel_id=1, source_target_pairs={{0,2},{2,0},{4,6},{6,4},{8,10},{10,8},{12,14},{14,12},{16,18},{18,... | collective-permute-start | bytes 3538952 | tf_op jit(solution)/shard_map/ppermute | solution.py:516
  263.5 7.6 %collective-permute-start.20 = (bf16[24,1536]{1,0:T(8,128)(2,1)S(1)}, bf16[24,1536]{1,0:T(8,128)(2,1)S(1)}, u32[]{:S(2)}, u32[]{:S(2)}) collective-permute-start(bf16[24,1536]{1,0:T(8,128)(2,1)S(1)} %constant_dynamic-slice_fusion.11), channel_id=1, source_target_pairs={{0,16},{2,18},{4,20},{6,22},{8,24},{10,26},{12,28},{14,30},{16,0},... | collective-permute-start | bytes 221192 | tf_op jit(solution)/shard_map/ppermute | solution.py:516
  263.6 58.1 %collective-permute-start.49 = (bf16[768,768]{1,0:T(8,128)(2,1)S(1)}, bf16[768,768]{1,0:T(8,128)(2,1)S(1)}, u32[]{:S(2)}, u32[]{:S(2)}) collective-permute-start(bf16[768,768]{1,0:T(8,128)(2,1)S(1)} %pad_maximum_fusion.7), channel_id=1, source_target_pairs={{0,2},{2,0},{4,6},{6,4},{8,10},{10,8},{12,14},{14,12},{16,18},{18,... | collective-permute-start | bytes 3538952 | tf_op jit(solution)/shard_map/ppermute | solution.py:516
  271.1 5.3 %collective-permute-start.21 = (bf16[24,1536]{1,0:T(8,128)(2,1)S(1)}, bf16[24,1536]{1,0:T(8,128)(2,1)S(1)}, u32[]{:S(2)}, u32[]{:S(2)}) collective-permute-start(bf16[24,1536]{1,0:T(8,128)(2,1)S(1)} %add_convert_fusion.20), channel_id=1, source_target_pairs={{0,16},{2,18},{4,20},{6,22},{8,24},{10,26},{12,28},{14,30},{16,0},... | collective-permute-start | bytes 221192 | tf_op jit(solution)/shard_map/ppermute | solution.py:516
  272.8 11.0 %collective-permute-start.27 = (bf16[192,1536]{1,0:T(8,128)(2,1)S(1)}, bf16[192,1536]{1,0:T(8,128)(2,1)S(1)}, u32[]{:S(2)}, u32[]{:S(2)}) collective-permute-start(bf16[192,1536]{1,0:T(8,128)(2,1)S(1)} %constant_dynamic-slice_fusion.9), channel_id=1, source_target_pairs={{0,4},{2,6},{4,0},{6,2},{8,12},{10,14},{12,8},{14,10},{16,20},{18,... | collective-permute-start | bytes 1769480 | tf_op jit(solution)/shard_map/ppermute | solution.py:516
  276.4 9.0 %collective-permute-start.22 = (bf16[48,1536]{1,0:T(8,128)(2,1)S(1)}, bf16[48,1536]{1,0:T(8,128)(2,1)S(1)}, u32[]{:S(2)}, u32[]{:S(2)}) collective-permute-start(bf16[48,1536]{1,0:T(8,128)(2,1)S(1)} %pad_maximum_fusion.17), channel_id=1, source_target_pairs={{0,8},{2,10},{4,12},{6,14},{8,0},{10,2},{12,4},{14,6},{16,24},{18,... | collective-permute-start | bytes 442376 | tf_op jit(solution)/shard_map/ppermute | solution.py:516
  284.0 6.8 %collective-permute-start.28 = (bf16[96,1536]{1,0:T(8,128)(2,1)S(1)}, bf16[96,1536]{1,0:T(8,128)(2,1)S(1)}, u32[]{:S(2)}, u32[]{:S(2)}) collective-permute-start(bf16[96,1536]{1,0:T(8,128)(2,1)S(1)} %constant_dynamic-slice_fusion.8), channel_id=1, source_target_pairs={{0,1},{1,0},{2,3},{3,2},{4,5},{5,4},{6,7},{7,6},{8,9},{9,8},{10,11... | collective-permute-start | bytes 884744 | tf_op jit(solution)/shard_map/ppermute | solution.py:516
  291.1 5.2 %collective-permute-start.29 = (bf16[48,1536]{1,0:T(8,128)(2,1)S(1)}, bf16[48,1536]{1,0:T(8,128)(2,1)S(1)}, u32[]{:S(2)}, u32[]{:S(2)}) collective-permute-start(bf16[48,1536]{1,0:T(8,128)(2,1)S(1)} %constant_dynamic-slice_fusion.7), channel_id=1, source_target_pairs={{0,8},{2,10},{4,12},{6,14},{8,0},{10,2},{12,4},{14,6},{16,24},{18,... | collective-permute-start | bytes 442376 | tf_op jit(solution)/shard_map/ppermute | solution.py:516
  291.7 6.9 %collective-permute-start.23 = (bf16[96,1536]{1,0:T(8,128)(2,1)S(1)}, bf16[96,1536]{1,0:T(8,128)(2,1)S(1)}, u32[]{:S(2)}, u32[]{:S(2)}) collective-permute-start(bf16[96,1536]{1,0:T(8,128)(2,1)S(1)} %pad_maximum_fusion.13), channel_id=1, source_target_pairs={{0,4},{2,6},{4,0},{6,2},{8,12},{10,14},{12,8},{14,10},{16,20},{18,... | collective-permute-start | bytes 884744 | tf_op jit(solution)/shard_map/ppermute | solution.py:516
  296.4 6.1 %collective-permute-start.30 = (bf16[24,1536]{1,0:T(8,128)(2,1)S(1)}, bf16[24,1536]{1,0:T(8,128)(2,1)S(1)}, u32[]{:S(2)}, u32[]{:S(2)}) collective-permute-start(bf16[24,1536]{1,0:T(8,128)(2,1)S(1)} %constant_dynamic-slice_fusion.6), channel_id=1, source_target_pairs={{0,16},{2,18},{4,20},{6,22},{8,24},{10,26},{12,28},{14,30},{16,0},... | collective-permute-start | bytes 221192 | tf_op jit(solution)/shard_map/ppermute | solution.py:516
  302.6 5.5 %collective-permute-start.31 = (bf16[24,1536]{1,0:T(8,128)(2,1)S(1)}, bf16[24,1536]{1,0:T(8,128)(2,1)S(1)}, u32[]{:S(2)}, u32[]{:S(2)}) collective-permute-start(bf16[24,1536]{1,0:T(8,128)(2,1)S(1)} %add_convert_fusion.19), channel_id=1, source_target_pairs={{0,16},{2,18},{4,20},{6,22},{8,24},{10,26},{12,28},{14,30},{16,0},... | collective-permute-start | bytes 221192 | tf_op jit(solution)/shard_map/ppermute | solution.py:516
  304.8 16.6 %collective-permute-start.24 = (bf16[192,1536]{1,0:T(8,128)(2,1)S(1)}, bf16[192,1536]{1,0:T(8,128)(2,1)S(1)}, u32[]{:S(2)}, u32[]{:S(2)}) collective-permute-start(bf16[192,1536]{1,0:T(8,128)(2,1)S(1)} %pad_maximum_fusion.9), channel_id=1, source_target_pairs={{0,1},{1,0},{2,3},{3,2},{4,5},{5,4},{6,7},{7,6},{8,9},{9,8},{10,11... | collective-permute-start | bytes 1769480 | tf_op jit(solution)/shard_map/ppermute | solution.py:516
  308.1 5.2 %collective-permute-start.32 = (bf16[48,1536]{1,0:T(8,128)(2,1)S(1)}, bf16[48,1536]{1,0:T(8,128)(2,1)S(1)}, u32[]{:S(2)}, u32[]{:S(2)}) collective-permute-start(bf16[48,1536]{1,0:T(8,128)(2,1)S(1)} %pad_maximum_fusion.18), channel_id=1, source_target_pairs={{0,8},{2,10},{4,12},{6,14},{8,0},{10,2},{12,4},{14,6},{16,24},{18,... | collective-permute-start | bytes 442376 | tf_op jit(solution)/shard_map/ppermute | solution.py:516
  313.4 6.8 %collective-permute-start.33 = (bf16[96,1536]{1,0:T(8,128)(2,1)S(1)}, bf16[96,1536]{1,0:T(8,128)(2,1)S(1)}, u32[]{:S(2)}, u32[]{:S(2)}) collective-permute-start(bf16[96,1536]{1,0:T(8,128)(2,1)S(1)} %pad_maximum_fusion.14), channel_id=1, source_target_pairs={{0,1},{1,0},{2,3},{3,2},{4,5},{5,4},{6,7},{7,6},{8,9},{9,8},{10,11... | collective-permute-start | bytes 884744 | tf_op jit(solution)/shard_map/ppermute | solution.py:516
  320.3 9.9 %collective-permute-start.34 = (bf16[192,1536]{1,0:T(8,128)(2,1)S(1)}, bf16[192,1536]{1,0:T(8,128)(2,1)S(1)}, u32[]{:S(2)}, u32[]{:S(2)}) collective-permute-start(bf16[192,1536]{1,0:T(8,128)(2,1)S(1)} %pad_maximum_fusion.10), channel_id=1, source_target_pairs={{0,4},{2,6},{4,0},{6,2},{8,12},{10,14},{12,8},{14,10},{16,20},{18,... | collective-permute-start | bytes 1769480 | tf_op jit(solution)/shard_map/ppermute | solution.py:516
  321.6 11.5 %collective-permute-start.25 = (bf16[384,1536]{1,0:T(8,128)(2,1)S(1)}, bf16[384,1536]{1,0:T(8,128)(2,1)S(1)}, u32[]{:S(2)}, u32[]{:S(2)}) collective-permute-start(bf16[384,1536]{1,0:T(8,128)(2,1)S(1)} %pad_maximum_fusion.4), channel_id=1, source_target_pairs={{0,2},{2,0},{4,6},{6,4},{8,10},{10,8},{12,14},{14,12},{16,18},{18,... | collective-permute-start | bytes 3538952 | tf_op jit(solution)/shard_map/ppermute | solution.py:516
  330.5 4.6 %collective-permute-start.35 = (bf16[384,1536]{1,0:T(8,128)(2,1)S(1)}, bf16[384,1536]{1,0:T(8,128)(2,1)S(1)}, u32[]{:S(2)}, u32[]{:S(2)}) collective-permute-start(bf16[384,1536]{1,0:T(8,128)(2,1)S(1)} %pad_maximum_fusion.5), channel_id=1, source_target_pairs={{0,2},{2,0},{4,6},{6,4},{8,10},{10,8},{12,14},{14,12},{16,18},{18,... | collective-permute-start | bytes 3538952 | tf_op jit(solution)/shard_map/ppermute | solution.py:516
  (50 other events, 320.6 us)
